TPU v7x, 32 devices: a whole 2x2x4 slice. The times are simulated.
32 devices in a mesh: dp: 4 (over y, core), expert: 2 (over x), tensor: 4 (over z).
Axes of the slice: x: 2, y: 2, z: 4, core: 2. Of those that a mesh axis runs over, the one named last changes fastest.
Arguments:
- inputs: bfloat16 [1576, 768], P(('dp', 'expert')), may hold values from -6 to 6
- first_gain: float32 [768], replicated, may hold values from 0.5 to 1.5
- first_bias: float32 [768], replicated, may hold values from -2 to 2
- attention_in: bfloat16 [3, 768, 768], P(None, None, 'tensor')
- attention_out: bfloat16 [768, 768], P('tensor'), may hold values from -0.875 to 0.875
- second_gain: float32 [768], replicated, may hold values from 0.5 to 1.5
- second_bias: float32 [768], replicated, may hold values from -2 to 2
- router_weight: float32 [768, 4], replicated
- expert_in: bfloat16 [4, 768, 3072], P('expert', None, 'tensor'), may hold values from -0.21875 to 0.21875
- expert_out: bfloat16 [4, 3072, 768], P('expert', 'tensor'), may hold values from -1.75 to 1.75
- expert_ids: int32 [1576, 2], P(('dp', 'expert')), may hold values from 0 to 3, as said below
- slot_index: int32 [1576, 2], P(('dp', 'expert')), may hold values from 0 to 98, as said below
- cotangent: bfloat16 [1576, 768], P(('dp', 'expert')), may hold values from -6 to 6
Outputs:
- layer_out: float32 [1576, 768], P(('dp', 'expert'))
- input_grad: float32 [1576, 768], P(('dp', 'expert'))
- first_gain_grad: float32 [768], P(('dp', 'expert'))
- first_bias_grad: float32 [768], P(('dp', 'expert'))
- attention_in_grad: float32 [3, 768, 768], P(None, ('dp', 'expert'), 'tensor')
- attention_out_grad: float32 [768, 768], P('tensor', ('dp', 'expert'))
- second_gain_grad: float32 [768], P(('dp', 'expert'))
- second_bias_grad: float32 [768], P(('dp', 'expert'))
- router_grad: float32 [768, 4], P(('dp', 'expert'))
- expert_in_grad: float32 [4, 768, 3072], P('expert', 'dp', 'tensor')
- expert_out_grad: float32 [4, 3072, 768], P('expert', 'tensor', 'dp')
Inputs may be any that keep to these rules, and one draw needn't show every extreme that they name: `expert_ids`: the two experts of a token differ. `slot_index`: among the 197 tokens of one index of dp and expert, the choices naming one expert hold slots 0, 1, 2 and so on, all first choices before all second choices, rows in order within each; a choice ranked 98 or later holds 98 and is dropped. Some expert fills all 98 slots from every index of dp and expert.
All inputs are finite; a program needn't handle non-finite values.
Results may differ from a plain program's by a relative error of at most 0.02.
Values may be sent and summed in bfloat16 or wider, within the bound.
A program may use at most 128 MiB of HBM per device.

v0:
```python
import math

import jax
import jax.numpy as jnp
from jax import lax
from jax.sharding import PartitionSpec as P

HEAD_DIM = 64
SEQ = 197


EPS = 1e-06
GELU_C = math.sqrt(2.0 / math.pi)


def cut_along(shard, dim, devices):
    shape = shard.shape
    tiles = shard.reshape(*shape[:dim], devices, shape[dim] // devices, *shape[dim + 1 :])
    return jnp.moveaxis(tiles, dim, 0)


def sent_and_summed(shard, axis, dim):
    devices = lax.axis_size(axis)
    tiles = lax.all_to_all(cut_along(shard, dim, devices), axis, 0, 0, tiled=True)
    return jnp.sum(tiles.astype(jnp.float32), axis=0)


def sent_together(arrays, axis, dim, along):
    widths = [math.prod(a.shape[along:]) for a in arrays]
    both = jnp.concatenate(
        [a.reshape(*a.shape[:along], w) for a, w in zip(arrays, widths)], axis=along
    )
    out = sent_and_summed(both, axis, dim)
    tiles = jnp.split(out, [sum(widths[:k]) for k in range(1, len(widths))], axis=along)
    return tuple((b.reshape(*out.shape[:along], *a.shape[along:]) for a, b in zip(arrays, tiles)))


def normalize(values):
    centre = jnp.mean(values, axis=-1, keepdims=True)
    centred = values - centre
    spread = jnp.mean(centred * centred, axis=-1, keepdims=True)
    scale = lax.rsqrt(spread + EPS)
    return (centred * scale, scale)


def norm_back(grad_out, normed, scale, gain):
    scaled = grad_out * gain
    first_mean = jnp.mean(scaled, axis=-1, keepdims=True)
    second_mean = jnp.mean(scaled * normed, axis=-1, keepdims=True)
    return scale * (scaled - first_mean - normed * second_mean)


def gelu_parts(pre):
    inner = GELU_C * (pre + 0.044715 * pre * pre * pre)
    tangent = jnp.tanh(inner)
    value = 0.5 * pre * (1.0 + tangent)
    slope = 0.5 * (1.0 + tangent) + 0.5 * pre * (1.0 - tangent * tangent) * GELU_C * (
        1.0 + 3.0 * 0.044715 * pre * pre
    )
    return (value, slope)


def per_device(
    inputs,
    first_gain,
    first_bias,
    attention_in,
    attention_out,
    second_gain,
    second_bias,
    router_weight,
    expert_in,
    expert_out,
    expert_ids,
    slot_index,
    cotangent,
):
    tokens_here = inputs.shape[0]
    model_width = inputs.shape[1]
    images = tokens_here // SEQ
    local_width = attention_in.shape[2]
    local_heads = local_width // HEAD_DIM
    owners = lax.axis_size("expert")
    experts_here = expert_in.shape[0]
    experts_all = experts_here * owners
    capacity = (2 * tokens_here - 1) // experts_all
    scaling = HEAD_DIM ** (-0.5)

    def split_heads(matrix):
        return matrix.reshape(images, SEQ, local_heads, HEAD_DIM)

    x_full = inputs.astype(jnp.float32)
    normed1, scale1 = normalize(x_full)
    first = (normed1 * first_gain + first_bias).astype(jnp.bfloat16)
    project = [
        jnp.dot(first, attention_in[which], preferred_element_type=jnp.float32).astype(jnp.bfloat16)
        for which in range(3)
    ]
    query_h, keys_h, values_h = [split_heads(part) for part in project]
    scores = (
        jnp.einsum("iqhd,ikhd->ihqk", query_h, keys_h, preferred_element_type=jnp.float32) * scaling
    )
    peak = jnp.max(scores, axis=-1, keepdims=True)
    logsum = peak[..., 0] + jnp.log(jnp.sum(jnp.exp(scores - peak), axis=-1))
    weights = jnp.exp(scores - logsum[..., None]).astype(jnp.bfloat16)
    context_h = jnp.einsum(
        "ihqk,ikhd->iqhd", weights, values_h, preferred_element_type=jnp.float32
    ).astype(jnp.bfloat16)
    context = context_h.reshape(tokens_here, local_width)
    partial_attn = jnp.dot(context, attention_out, preferred_element_type=jnp.float32)
    attended = lax.psum(partial_attn, "tensor")
    resid = x_full + attended
    normed2, scale2 = normalize(resid)
    second = (normed2 * second_gain + second_bias).astype(jnp.bfloat16)
    logits = jnp.dot(second.astype(jnp.float32), router_weight, precision=lax.Precision.HIGHEST)
    route = jax.nn.softmax(logits, axis=-1)
    valid = (slot_index < capacity).astype(jnp.float32)
    choose = (expert_ids[:, :, None] == jnp.arange(experts_all, dtype=jnp.int32)).astype(
        jnp.float32
    )
    gate = jnp.sum(route[:, None, :] * choose, axis=-1) * valid
    target = jnp.where(slot_index < capacity, expert_ids * capacity + slot_index, -1)
    chosen = (target[:, :, None] == jnp.arange(experts_all * capacity, dtype=jnp.int32)).astype(
        jnp.bfloat16
    )
    placing = jnp.sum(chosen, axis=1)
    sendbuf = jnp.einsum("rq,rd->qd", placing, second, preferred_element_type=jnp.float32).astype(
        jnp.bfloat16
    )
    sendbuf = sendbuf.reshape(owners, experts_here, capacity, model_width)
    received = lax.all_to_all(sendbuf, "expert", split_axis=0, concat_axis=0, tiled=True)
    pre = jnp.einsum("skcd,kdf->skcf", received, expert_in, preferred_element_type=jnp.float32)
    value, slope = gelu_parts(pre)
    hidden = value.astype(jnp.bfloat16)
    partial_value = jnp.einsum(
        "skcf,kfd->skcd", hidden, expert_out, preferred_element_type=jnp.float32
    )
    summed = lax.psum(partial_value, "tensor")
    returned = lax.all_to_all(
        summed.astype(jnp.bfloat16), "expert", split_axis=0, concat_axis=0, tiled=True
    )
    outcome = (returned, received, hidden, slope)
    returned = outcome[0]
    received = outcome[1]
    outputs_flat = returned.reshape(experts_all * capacity, model_width)
    picked = jnp.einsum("rjq,qd->rjd", chosen, outputs_flat, preferred_element_type=jnp.float32)
    layer_out = resid + jnp.sum(gate[..., None] * picked, axis=1)
    grad_out = cotangent.astype(jnp.float32)
    gate_grad = jnp.sum(grad_out[:, None, :] * picked, axis=-1) * valid
    slot_gate = jnp.einsum(
        "rjq,rj->q", chosen.astype(jnp.float32), gate, precision=lax.Precision.HIGHEST
    )
    slotted = jnp.einsum("rq,rd->qd", placing, cotangent, preferred_element_type=jnp.float32)
    grad_send = (
        (slot_gate[:, None] * slotted)
        .astype(jnp.bfloat16)
        .reshape(owners, experts_here, capacity, model_width)
    )
    grad_recv = lax.all_to_all(grad_send, "expert", split_axis=0, concat_axis=0, tiled=True)
    hidden = outcome[2]
    slope = outcome[3]
    hidden_grad = jnp.einsum(
        "skcd,kfd->skcf", grad_recv, expert_out, preferred_element_type=jnp.float32
    )
    pre_grad = (hidden_grad * slope).astype(jnp.bfloat16)
    local_out_grad = jnp.einsum(
        "skcf,skcd->kfd", hidden, grad_recv, preferred_element_type=jnp.float32
    )
    local_in_grad = jnp.einsum(
        "skcd,skcf->kdf", received, pre_grad, preferred_element_type=jnp.float32
    )
    partial_back = jnp.einsum(
        "skcf,kdf->skcd", pre_grad, expert_in, preferred_element_type=jnp.float32
    )
    back_sum = lax.psum(partial_back.astype(jnp.bfloat16), "tensor")
    back_home = lax.all_to_all(back_sum, "expert", split_axis=0, concat_axis=0, tiled=True)
    back_rows = jnp.einsum(
        "rjq,qd->rd",
        chosen,
        back_home.reshape(experts_all * capacity, model_width),
        preferred_element_type=jnp.float32,
    )
    expert_in_grad, expert_out_grad = (
        lax.psum_scatter(
            local_in_grad.astype(jnp.bfloat16), "dp", scatter_dimension=1, tiled=True
        ).astype(jnp.float32),
        lax.psum_scatter(
            local_out_grad.astype(jnp.bfloat16), "dp", scatter_dimension=2, tiled=True
        ).astype(jnp.float32),
    )
    route_grad = jnp.sum(gate_grad[:, :, None] * choose, axis=1)
    logit_grad = route * (route_grad - jnp.sum(route * route_grad, axis=-1, keepdims=True))
    local_router = jnp.dot(
        second.astype(jnp.float32).T, logit_grad, precision=lax.Precision.HIGHEST
    )
    second_grad = back_rows + jnp.dot(logit_grad, router_weight.T, precision=lax.Precision.HIGHEST)
    local_second_gain = jnp.sum(second_grad * normed2, axis=0)
    local_second_bias = jnp.sum(second_grad, axis=0)
    resid_grad = grad_out + norm_back(second_grad, normed2, scale2, second_gain)
    resid_low = resid_grad.astype(jnp.bfloat16)
    local_attn_out = jnp.einsum("rh,rd->hd", context, resid_low, preferred_element_type=jnp.float32)
    context_grad = jnp.einsum(
        "rd,hd->rh", resid_low, attention_out, preferred_element_type=jnp.float32
    ).astype(jnp.bfloat16)
    context_g = split_heads(context_grad)
    probs = jnp.exp(scores - logsum[..., None])
    values_grad = jnp.einsum(
        "ihqk,iqhd->ikhd", weights, context_g, preferred_element_type=jnp.float32
    ).astype(jnp.bfloat16)
    probs_grad = jnp.einsum(
        "iqhd,ikhd->ihqk", context_g, values_h, preferred_element_type=jnp.float32
    )
    delta = jnp.transpose(
        jnp.sum(context_g.astype(jnp.float32) * context_h.astype(jnp.float32), axis=-1), (0, 2, 1)
    )
    score_grad = (probs * (probs_grad - delta[..., None]) * scaling).astype(jnp.bfloat16)
    query_grad = jnp.einsum(
        "ihqk,ikhd->iqhd", score_grad, keys_h, preferred_element_type=jnp.float32
    ).astype(jnp.bfloat16)
    keys_grad = jnp.einsum(
        "ihqk,iqhd->ikhd", score_grad, query_h, preferred_element_type=jnp.float32
    ).astype(jnp.bfloat16)
    grads_flat = [
        part.reshape(tokens_here, local_width) for part in (query_grad, keys_grad, values_grad)
    ]
    local_attn_in = jnp.stack(
        [
            jnp.einsum("rd,rh->dh", first, part, preferred_element_type=jnp.float32)
            for part in grads_flat
        ]
    )
    partial_first = jnp.einsum(
        "rh,dh->rd", grads_flat[0], attention_in[0], preferred_element_type=jnp.float32
    )
    partial_first = partial_first + jnp.einsum(
        "rh,dh->rd", grads_flat[1], attention_in[1], preferred_element_type=jnp.float32
    )
    partial_first = partial_first + jnp.einsum(
        "rh,dh->rd", grads_flat[2], attention_in[2], preferred_element_type=jnp.float32
    )
    first_grad = lax.psum(partial_first.astype(jnp.bfloat16), "tensor").astype(jnp.float32)
    local_first_gain = jnp.sum(first_grad * normed1, axis=0)
    local_first_bias = jnp.sum(first_grad, axis=0)
    input_grad = resid_grad + norm_back(first_grad, normed1, scale1, first_gain)
    summed_shared = (
        sent_and_summed(local_attn_in.astype(jnp.bfloat16), ("dp", "expert"), 1),
        sent_and_summed(local_attn_out.astype(jnp.bfloat16), ("dp", "expert"), 1),
        *sent_together(
            (
                local_router.astype(jnp.bfloat16),
                local_first_gain.astype(jnp.bfloat16),
                local_first_bias.astype(jnp.bfloat16),
                local_second_gain.astype(jnp.bfloat16),
                local_second_bias.astype(jnp.bfloat16),
            ),
            ("dp", "expert"),
            0,
            1,
        ),
    )
    (
        attention_in_grad,
        attention_out_grad,
        router_grad,
        first_gain_grad,
        first_bias_grad,
        second_gain_grad,
        second_bias_grad,
    ) = summed_shared
    return (
        layer_out,
        input_grad,
        first_gain_grad,
        first_bias_grad,
        attention_in_grad,
        attention_out_grad,
        second_gain_grad,
        second_bias_grad,
        router_grad,
        expert_in_grad,
        expert_out_grad,
    )


def solution(mesh):
    in_specs = (
        P(("dp", "expert"), None),
        P(),
        P(),
        P(None, None, "tensor"),
        P("tensor", None),
        P(),
        P(),
        P(),
        P("expert", None, "tensor"),
        P("expert", "tensor", None),
        P(("dp", "expert"), None),
        P(("dp", "expert"), None),
        P(("dp", "expert"), None),
    )
    out_specs = (
        P(("dp", "expert"), None),
        P(("dp", "expert"), None),
        P(("dp", "expert")),
        P(("dp", "expert")),
        P(None, ("dp", "expert"), "tensor"),
        P("tensor", ("dp", "expert")),
        P(("dp", "expert")),
        P(("dp", "expert")),
        P(("dp", "expert"), None),
        P("expert", "dp", "tensor"),
        P("expert", "tensor", "dp"),
    )
    return jax.shard_map(
        per_device, mesh=mesh, in_specs=in_specs, out_specs=out_specs, check_vma=False
    )
```

profile of v0, /device:TPU:0, one launch (start us, length us, event | category | flops | bytes accessed | tf_op | source)
XLA Modules:
  0.0 338.7 jit_solution(17743377087618630051)
XLA Ops:
  15.5 42.5 %all-reduce.5.cloned.1.call-done = f32[197,768]{1,0:T(8,128)} async-done(((f32[197,768]{1,0:T(8,128)}), f32[197,768]{1,0:T(8,128)}) %all-reduce.5.cloned.1.call-update) | async-done | bytes 605200 | tf_op jit(solution)/shard_map/psum | solution.py:111
  63.6 2.4 copy.130
  66.0 4.2 %all-to-all-start = ((bf16[2,2,98,768]{3,1,2,0:T(2,128)(2,1)}), bf16[2,2,98,768]{3,1,2,0:T(2,128)(2,1)}, u32[]{:S(2)}, u32[]{:S(2)}) async-start(bf16[2,2,98,768]{3,1,2,0:T(2,128)(2,1)} %copy.130), calls=%async_computation | async-start | bytes 1204224 | tf_op jit(solution)/shard_map/all_to_all | solution.py:131
  74.9 2.4 copy.134
  78.8 4.3 %all-to-all-start.2 = ((bf16[2,2,98,768]{3,1,2,0:T(2,128)(2,1)}), bf16[2,2,98,768]{3,1,2,0:T(2,128)(2,1)}, u32[]{:S(2)}, u32[]{:S(2)}) async-start(bf16[2,2,98,768]{3,1,2,0:T(2,128)(2,1)} %copy.134), calls=%async_computation.2 | async-start | bytes 1204224 | tf_op jit(solution)/shard_map/all_to_all | solution.py:159
  83.1 2.5 fusion.14
  89.5 47.3 %all-reduce.10 = bf16[2,2,98,768]{3,1,2,0:T(2,128)(2,1)} all-reduce(f32[2,2,98,768]{3,1,2,0:T(2,128)} %bitcast.163), channel_id=1, replica_groups=mesh['dp'=4,'expert'=2,'tensor'=4] {'tensor'}, use_global_device_ids=true, to_apply=%region_11.12 | all-reduce | flops 301056 | bytes 1806336 | tf_op jit(solution)/shard_map/psum | solution.py:138
  136.7 4.3 %all-to-all-start.1 = ((bf16[2,2,98,768]{3,1,2,0:T(2,128)(2,1)}), bf16[2,2,98,768]{3,1,2,0:T(2,128)(2,1)}, u32[]{:S(2)}, u32[]{:S(2)}) async-start(bf16[2,2,98,768]{3,1,2,0:T(2,128)(2,1)} %all-reduce.10), calls=%async_computation.1 | async-start | bytes 1204224 | tf_op jit(solution)/shard_map/all_to_all | solution.py:139
  141.1 2.9 fusion.17
  152.4 2.8 multiply_reduce_fusion
  155.3 31.0 %all-reduce.7.cloned.1.call-done = bf16[2,2,98,768]{3,2,0,1:T(8,128)(2,1)} async-done(((bf16[2,2,98,768]{3,2,0,1:T(8,128)(2,1)}), bf16[2,2,98,768]{3,2,0,1:T(8,128)(2,1)}) %all-reduce.7.cloned.1.call-update) | async-done | bytes 602128 | tf_op jit(solution)/shard_map/psum | solution.py:175
  186.3 2.4 copy.136
  188.6 4.2 %all-to-all-start.3 = ((bf16[2,2,98,768]{3,1,2,0:T(2,128)(2,1)}), bf16[2,2,98,768]{3,1,2,0:T(2,128)(2,1)}, u32[]{:S(2)}, u32[]{:S(2)}) async-start(bf16[2,2,98,768]{3,1,2,0:T(2,128)(2,1)} %copy.136), calls=%async_computation.3 | async-start | bytes 1204224 | tf_op jit(solution)/shard_map/all_to_all | solution.py:176
  194.7 6.8 %all-to-all-done.3 = bf16[2,2,98,768]{3,1,2,0:T(2,128)(2,1)} async-done(((bf16[2,2,98,768]{3,1,2,0:T(2,128)(2,1)}), bf16[2,2,98,768]{3,1,2,0:T(2,128)(2,1)}, u32[]{:S(2)}, u32[]{:S(2)}) %all-to-all-start.3) | async-done | bytes 602144 | tf_op jit(solution)/shard_map/all_to_all | solution.py:176
  212.7 3.3 bitcast_convert_fusion.1
  216.1 3.8 %bitcast_convert_fusion = bf16[2,768,768]{1,2,0:T(8,128)(2,1)} fusion(bf16[2,2,98,768]{3,1,2,0:T(2,128)(2,1)} %all-to-all-done.2, f32[2,2,98,768]{3,2,0,1:T(8,128)} %copy-done.14), kind=kOutput, calls=%fused_computation | convolution fusion | flops 466311168 | bytes 4165632 | tf_op jit(solution)/shard_map/skcf,skcd->kfd/dot_general | solution.py:166
  226.0 4.1 %all-to-all-start.6 = ((bf16[8,192,96]{2,1,0:T(8,128)(2,1)}), bf16[8,192,96]{2,1,0:T(8,128)(2,1)}, u32[]{:S(2)}, u32[]{:S(2)}) async-start(bf16[8,192,96]{2,1,0:T(8,128)(2,1)} %bitcast.164), calls=%async_computation.6 | async-start | bytes 786432 | tf_op jit(solution)/shard_map/all_to_all | solution.py:24
  231.6 6.3 %all-to-all-done.6 = bf16[8,192,96]{2,1,0:T(8,128)(2,1)} async-done(((bf16[8,192,96]{2,1,0:T(8,128)(2,1)}), bf16[8,192,96]{2,1,0:T(8,128)(2,1)}, u32[]{:S(2)}, u32[]{:S(2)}) %all-to-all-start.6) | async-done | bytes 294944 | tf_op jit(solution)/shard_map/all_to_all | solution.py:24
  239.5 8.2 %all-reduce.9.cloned.1.call-done = bf16[197,768]{1,0:T(8,128)(2,1)} async-done(((bf16[197,768]{1,0:T(8,128)(2,1)}), bf16[197,768]{1,0:T(8,128)(2,1)}) %all-reduce.9.cloned.1.call-update) | async-done | bytes 302608 | tf_op jit(solution)/shard_map/psum | solution.py:241
  251.6 3.6 %all-to-all-start.4 = ((bf16[8,96,8]{1,2,0:T(8,128)(2,1)}), bf16[8,96,8]{1,2,0:T(8,128)(2,1)S(1)}, u32[]{:S(2)}, u32[]{:S(2)}) async-start(bf16[8,96,8]{1,2,0:T(8,128)(2,1)} %concatenate.12), calls=%async_computation.4 | async-start | bytes 32768 | tf_op jit(solution)/shard_map/all_to_all | solution.py:24
  261.5 4.3 %all-to-all-start.5 = ((bf16[8,3,96,192]{3,2,1,0:T(8,128)(2,1)}), bf16[8,3,96,192]{3,2,1,0:T(8,128)(2,1)}, u32[]{:S(2)}, u32[]{:S(2)}) async-start(bf16[8,3,96,192]{3,2,1,0:T(8,128)(2,1)} %copy.150), calls=%async_computation.5 | async-start | bytes 2359296 | tf_op jit(solution)/shard_map/all_to_all | solution.py:24
  269.0 19.1 %all-to-all-done.5 = bf16[8,3,96,192]{3,2,1,0:T(8,128)(2,1)} async-done(((bf16[8,3,96,192]{3,2,1,0:T(8,128)(2,1)}), bf16[8,3,96,192]{3,2,1,0:T(8,128)(2,1)}, u32[]{:S(2)}, u32[]{:S(2)}) %all-to-all-start.5) | async-done | bytes 884768 | tf_op jit(solution)/shard_map/all_to_all | solution.py:24
  290.2 5.2 %reduce-scatter.3.cloned.1.call-done = bf16[2,192,768]{2,1,0:T(8,128)(2,1)} async-done(((bf16[2,768,768]{2,1,0:T(8,128)(2,1)}), bf16[2,192,768]{2,1,0:T(8,128)(2,1)}) %reduce-scatter.3.cloned.1.call-update) | async-done | bytes 589840 | tf_op jit(solution)/shard_map/reduce_scatter | solution.py:184
  297.6 32.4 %reduce-scatter.5.cloned.1.call-done = bf16[2,768,192]{1,2,0:T(8,128)(2,1)} async-done(((bf16[2,768,768]{1,2,0:T(8,128)(2,1)}), bf16[2,768,192]{1,2,0:T(8,128)(2,1)}) %reduce-scatter.5.cloned.1.call-update) | async-done | bytes 589840 | tf_op jit(solution)/shard_map/reduce_scatter | solution.py:187
  (178 shorter events, 74.1 us)
Async XLA Ops:
  7.2 79.5 %copy-start = (bf16[2,768,768]{2,1,0:T(8,128)(2,1)S(1)}, bf16[2,768,768]{2,1,0:T(8,128)(2,1)}, u32[]{:S(2)}) copy-start(bf16[2,768,768]{2,1,0:T(8,128)(2,1)} %param.22) | copy-start | bytes 7077892
  7.2 4.1 %copy-start.6 = (bf16[197,768]{1,0:T(8,128)(2,1)S(1)}, bf16[197,768]{1,0:T(8,128)(2,1)}, u32[]{:S(2)}) copy-start(bf16[197,768]{1,0:T(8,128)(2,1)} %param.13) | copy-start | bytes 907780
  7.2 4.1 %copy-start.17 = (bf16[3,768,192]{1,2,0:T(8,128)(2,1)S(1)}, bf16[3,768,192]{1,2,0:T(8,128)(2,1)}, u32[]{:S(2)}) copy-start(bf16[3,768,192]{1,2,0:T(8,128)(2,1)} %param.16) | copy-start | bytes 2654212
  7.2 50.8 %all-reduce.5.cloned.1.call-start = ((), (), s32[]{:S(2)}) async-start(), calls=%async_computation.9 | async-start | bytes 1228800 | tf_op jit(solution)/shard_map/psum | solution.py:111
  7.3 4.0 %copy-start.34 = (f32[768]{0:T(1024)S(1)}, f32[768]{0:T(1024)}, u32[]{:S(2)}) copy-start(f32[768]{0:T(1024)} %param.14) | copy-start | bytes 9220
  7.3 4.0 %copy-start.39 = (f32[768]{0:T(1024)S(1)}, f32[768]{0:T(1024)}, u32[]{:S(2)}) copy-start(f32[768]{0:T(1024)} %param.15) | copy-start | bytes 9220
  15.3 44.1 %copy-start.31 = (f32[768]{0:T(1024)S(1)}, f32[768]{0:T(1024)}, u32[]{:S(2)}) copy-start(f32[768]{0:T(1024)} %param.18) | copy-start | bytes 9220
  15.3 44.1 %copy-start.38 = (f32[768]{0:T(1024)S(1)}, f32[768]{0:T(1024)}, u32[]{:S(2)}) copy-start(f32[768]{0:T(1024)} %param.19) | copy-start | bytes 9220
  15.5 44.2 %copy-start.30 = (f32[768,4]{0,1:T(4,128)S(1)}, f32[768,4]{0,1:T(4,128)}, u32[]{:S(2)}) copy-start(f32[768,4]{0,1:T(4,128)} %param.20) | copy-start | bytes 36868
  66.0 12.8 %all-to-all-start = ((bf16[2,2,98,768]{3,1,2,0:T(2,128)(2,1)}), bf16[2,2,98,768]{3,1,2,0:T(2,128)(2,1)}, u32[]{:S(2)}, u32[]{:S(2)}) async-start(bf16[2,2,98,768]{3,1,2,0:T(2,128)(2,1)} %copy.130), calls=%async_computation | async-start | bytes 1204224 | tf_op jit(solution)/shard_map/all_to_all | solution.py:131
  78.8 58.0 %all-to-all-start.2 = ((bf16[2,2,98,768]{3,1,2,0:T(2,128)(2,1)}), bf16[2,2,98,768]{3,1,2,0:T(2,128)(2,1)}, u32[]{:S(2)}, u32[]{:S(2)}) async-start(bf16[2,2,98,768]{3,1,2,0:T(2,128)(2,1)} %copy.134), calls=%async_computation.2 | async-start | bytes 1204224 | tf_op jit(solution)/shard_map/all_to_all | solution.py:159
  136.7 11.6 %all-to-all-start.1 = ((bf16[2,2,98,768]{3,1,2,0:T(2,128)(2,1)}), bf16[2,2,98,768]{3,1,2,0:T(2,128)(2,1)}, u32[]{:S(2)}, u32[]{:S(2)}) async-start(bf16[2,2,98,768]{3,1,2,0:T(2,128)(2,1)} %all-reduce.10), calls=%async_computation.1 | async-start | bytes 1204224 | tf_op jit(solution)/shard_map/all_to_all | solution.py:139
  141.0 45.3 %all-reduce.7.cloned.1.call-start = ((), (), s32[]{:S(2)}) async-start(), calls=%async_computation.10 | async-start | bytes 1277952 | tf_op jit(solution)/shard_map/psum | solution.py:175
  188.6 12.9 %all-to-all-start.3 = ((bf16[2,2,98,768]{3,1,2,0:T(2,128)(2,1)}), bf16[2,2,98,768]{3,1,2,0:T(2,128)(2,1)}, u32[]{:S(2)}, u32[]{:S(2)}) async-start(bf16[2,2,98,768]{3,1,2,0:T(2,128)(2,1)} %copy.136), calls=%async_computation.3 | async-start | bytes 1204224 | tf_op jit(solution)/shard_map/all_to_all | solution.py:176
  192.9 54.9 %all-reduce.9.cloned.1.call-start = ((), (), s32[]{:S(2)}) async-start(), calls=%async_computation.11 | async-start | bytes 614400 | tf_op jit(solution)/shard_map/psum | solution.py:241
  212.7 82.8 %reduce-scatter.3.cloned.1.call-start = ((), (), s32[]{:S(2)}) async-start(), calls=%async_computation.12 | async-start | bytes 2949120 | tf_op jit(solution)/shard_map/reduce_scatter | solution.py:184
  216.1 113.9 %reduce-scatter.5.cloned.1.call-start = ((), (), s32[]{:S(2)}) async-start(), calls=%async_computation.13 | async-start | bytes 2949120 | tf_op jit(solution)/shard_map/reduce_scatter | solution.py:187
  224.1 23.6 %copy-start.35 = (f32[768]{0:T(1024)S(1)}, f32[768]{0:T(1024)}, u32[]{:S(2)}) copy-start(f32[768]{0:T(1024)} %param.14) | copy-start | bytes 9220
  224.1 23.6 %copy-start.37 = (f32[197]{0:T(256)S(1)}, f32[197]{0:T(256)}, u32[]{:S(2)}) copy-start(f32[197]{0:T(256)} %copy-done.36) | copy-start | bytes 2368
  224.1 23.6 %copy-start.40 = (f32[768]{0:T(1024)S(1)}, f32[768]{0:T(1024)}, u32[]{:S(2)}) copy-start(f32[768]{0:T(1024)} %param.15) | copy-start | bytes 9220
  226.0 11.9 %all-to-all-start.6 = ((bf16[8,192,96]{2,1,0:T(8,128)(2,1)}), bf16[8,192,96]{2,1,0:T(8,128)(2,1)}, u32[]{:S(2)}, u32[]{:S(2)}) async-start(bf16[8,192,96]{2,1,0:T(8,128)(2,1)} %bitcast.164), calls=%async_computation.6 | async-start | bytes 786432 | tf_op jit(solution)/shard_map/all_to_all | solution.py:24
  239.5 18.9 %copy-start.20 = (bf16[3,64,197]{2,1,0:T(8,128)(2,1)S(1)}, bf16[3,64,197]{2,1,0:T(8,128)(2,1)}, u32[]{:S(2)}) copy-start(bf16[3,64,197]{2,1,0:T(8,128)(2,1)} %copy-done.19) | copy-start | bytes 226948
  251.6 9.9 %all-to-all-start.4 = ((bf16[8,96,8]{1,2,0:T(8,128)(2,1)}), bf16[8,96,8]{1,2,0:T(8,128)(2,1)S(1)}, u32[]{:S(2)}, u32[]{:S(2)}) async-start(bf16[8,96,8]{1,2,0:T(8,128)(2,1)} %concatenate.12), calls=%async_computation.4 | async-start | bytes 32768 | tf_op jit(solution)/shard_map/all_to_all | solution.py:24
  261.5 26.5 %all-to-all-start.5 = ((bf16[8,3,96,192]{3,2,1,0:T(8,128)(2,1)}), bf16[8,3,96,192]{3,2,1,0:T(8,128)(2,1)}, u32[]{:S(2)}, u32[]{:S(2)}) async-start(bf16[8,3,96,192]{3,2,1,0:T(8,128)(2,1)} %copy.150), calls=%async_computation.5 | async-start | bytes 2359296 | tf_op jit(solution)/shard_map/all_to_all | solution.py:24
  (29 other events, 46.4 us)
Sparse Core Ops, SparseCore 0:
  15.4 42.5 all-reduce.4
  146.6 39.5 all-reduce.6
  212.8 34.9 all-reduce.8
  250.1 45.2 reduce-scatter.2
  297.8 32.1 reduce-scatter.4
where the time goes:
time: 341 us; the launch traced here: 339 us
  waiting for transfers between devices  153 us (45%)
  blocking collectives  47.3 us (14%)
  matrix products  37.3 us (11%)
  local copies, waits for them, and re-layouts  36.2 us (11%)
  starting transfers between devices  29.3 us (9%)
  other arithmetic  21 us (6%)
  between operations  14.5 us (4%)
    psum x1, blocking collectives, per_device(): summed = lax.psum(partial_value, 'tensor')  47.3 us
    psum x1, waiting for transfers between devices, per_device(): attended = lax.psum(partial_attn, 'tensor')  42.5 us
    reduce_scatter x1, waiting for transfers between devices, per_device(): lax.psum_scatter(local_out_grad.astype(jnp.bfloat16), 'dp', scatter_dimen...  32.4 us
    psum x1, waiting for transfers between devices, per_device(): back_sum = lax.psum(partial_back.astype(jnp.bfloat16), 'tensor')  31 us
    all_to_all x3, waiting for transfers between devices, sent_and_summed(): lax.all_to_all(cut_along(shard, dim, devices), axis, 0, 0, tiled=True)  25.3 us
    all_to_all x3, starting transfers between devices, sent_and_summed(): lax.all_to_all(cut_along(shard, dim, devices), axis, 0, 0, tiled=True)  11.9 us
    psum x1, waiting for transfers between devices, per_device(): lax.psum(partial_first.astype(jnp.bfloat16), 'tensor').astype(jnp.float32)  8.2 us
    all_to_all x1, waiting for transfers between devices, per_device(): lax.all_to_all(back_sum, 'expert', split_axis=0, concat_axis=0, tiled=True)  6.82 us
  transfers between devices with their start and end apart: 12, of which 9 were waited for; matrix products, arithmetic and copies ran while one was open for 18% of the time, Pallas kernels for 0%

commit v1 on v0

v1 whole, which is shorter than its diff:
```python
import functools
import math

import jax
import jax.numpy as jnp
from jax import lax
from jax.experimental import pallas as pl
from jax.experimental.pallas import tpu as pltpu
from jax.sharding import PartitionSpec as P

HEAD_DIM = 64
SEQ = 197


EPS = 1e-06
GELU_C = math.sqrt(2.0 / math.pi)


def cut_along(shard, dim, devices):
    shape = shard.shape
    tiles = shard.reshape(*shape[:dim], devices, shape[dim] // devices, *shape[dim + 1 :])
    return jnp.moveaxis(tiles, dim, 0)


def sent_and_summed(shard, axis, dim):
    devices = lax.axis_size(axis)
    tiles = lax.all_to_all(cut_along(shard, dim, devices), axis, 0, 0, tiled=True)
    return jnp.sum(tiles.astype(jnp.float32), axis=0)


def sent_together(arrays, axis, dim, along):
    widths = [math.prod(a.shape[along:]) for a in arrays]
    both = jnp.concatenate(
        [a.reshape(*a.shape[:along], w) for a, w in zip(arrays, widths)], axis=along
    )
    out = sent_and_summed(both, axis, dim)
    tiles = jnp.split(out, [sum(widths[:k]) for k in range(1, len(widths))], axis=along)
    return tuple((b.reshape(*out.shape[:along], *a.shape[along:]) for a, b in zip(arrays, tiles)))


def normalize(values):
    centre = jnp.mean(values, axis=-1, keepdims=True)
    centred = values - centre
    spread = jnp.mean(centred * centred, axis=-1, keepdims=True)
    scale = lax.rsqrt(spread + EPS)
    return (centred * scale, scale)


def norm_back(grad_out, normed, scale, gain):
    scaled = grad_out * gain
    first_mean = jnp.mean(scaled, axis=-1, keepdims=True)
    second_mean = jnp.mean(scaled * normed, axis=-1, keepdims=True)
    return scale * (scaled - first_mean - normed * second_mean)


def gelu_parts(pre):
    inner = GELU_C * (pre + 0.044715 * pre * pre * pre)
    tangent = jnp.tanh(inner)
    value = 0.5 * pre * (1.0 + tangent)
    slope = 0.5 * (1.0 + tangent) + 0.5 * pre * (1.0 - tangent * tangent) * GELU_C * (
        1.0 + 3.0 * 0.044715 * pre * pre
    )
    return (value, slope)


MESH = pl.DeviceIdType.MESH


def greet(axes):
    barrier = pltpu.get_barrier_semaphore()
    peers = 0
    for axis in axes:
        devices = lax.axis_size(axis)
        me = lax.axis_index(axis)
        for k in range(1, devices):
            peer = lax.rem(me + k, devices)
            pl.semaphore_signal(barrier, inc=1, device_id={axis: peer}, device_id_type=MESH)
            peers += 1
    pl.semaphore_wait(barrier, peers)


def scatter_kernel(count, *refs):
    sources, targets = refs[:count], refs[count : 2 * count]
    send_sem, recv_sem = refs[2 * count :]
    devices = lax.axis_size("tensor")
    me = lax.axis_index("tensor")
    greet(("tensor",))
    copies = []
    for k in range(1, devices):
        peer = lax.rem(me + k, devices)
        for a in range(count):
            copy = pltpu.make_async_remote_copy(
                src_ref=sources[a].at[peer],
                dst_ref=targets[a].at[k],
                send_sem=send_sem.at[a, k],
                recv_sem=recv_sem.at[a, k],
                device_id={"tensor": peer},
                device_id_type=MESH,
            )
            copy.start()
            copies.append(copy)
    for a in range(count):
        targets[a][0] = sources[a][me]
    for copy in copies:
        copy.wait()


def scattered(arrays, collective_id):
    devices = lax.axis_size("tensor")
    count = len(arrays)
    return pl.pallas_call(
        functools.partial(scatter_kernel, count),
        out_shape=[jax.ShapeDtypeStruct(a.shape, a.dtype) for a in arrays],
        in_specs=[pl.BlockSpec(memory_space=pltpu.VMEM)] * count,
        out_specs=[pl.BlockSpec(memory_space=pltpu.VMEM)] * count,
        scratch_shapes=[
            pltpu.SemaphoreType.DMA((count, devices)),
            pltpu.SemaphoreType.DMA((count, devices)),
        ],
        compiler_params=pltpu.CompilerParams(collective_id=collective_id, has_side_effects=True),
        name=f"scatter{collective_id}",
    )(*arrays)


def gather_kernel(count, forward, *refs):
    sources, targets = refs[:count], refs[count : 2 * count]
    send_z, recv_z, send_x, recv_x = refs[2 * count :]
    devices = lax.axis_size("tensor")
    me = lax.axis_index("tensor")
    owners = lax.axis_size("expert") if forward else 1
    home = lax.axis_index("expert")
    greet(("tensor", "expert") if forward else ("tensor",))

    def across(a, k, source, place):
        copies = []
        for e in range(1, owners):
            copy = pltpu.make_async_remote_copy(
                src_ref=source,
                dst_ref=targets[a].at[e, place],
                send_sem=send_x.at[a, k, e],
                recv_sem=recv_x.at[a, k, e],
                device_id={"expert": lax.rem(home + e, owners)},
                device_id_type=MESH,
            )
            copy.start()
            copies.append(copy)
        return copies

    along = []
    for k in range(1, devices):
        peer = lax.rem(me + k, devices)
        for a in range(count):
            copy = pltpu.make_async_remote_copy(
                src_ref=sources[a],
                dst_ref=targets[a].at[0, me],
                send_sem=send_z.at[a, k],
                recv_sem=recv_z.at[a, k],
                device_id={"tensor": peer},
                device_id_type=MESH,
            )
            copy.start()
            along.append((a, k, copy))
    crossing = []
    for a in range(count):
        crossing += across(a, 0, sources[a], me)
    for a in range(count):
        targets[a][0, me] = sources[a][...]
    for a, k, copy in along:
        copy.wait()
        place = lax.rem(me + devices - k, devices)
        crossing += across(a, k, targets[a].at[0, place], place)
    for copy in crossing:
        copy.wait()


def gathered(arrays, collective_id, forward=False):
    devices = lax.axis_size("tensor")
    owners = lax.axis_size("expert") if forward else 1
    count = len(arrays)
    sems = [(count, devices)] * 2 + [(count, devices, owners)] * 2
    return pl.pallas_call(
        functools.partial(gather_kernel, count, forward),
        out_shape=[
            jax.ShapeDtypeStruct((owners, devices, *a.shape), a.dtype) for a in arrays
        ],
        in_specs=[pl.BlockSpec(memory_space=pltpu.VMEM)] * count,
        out_specs=[pl.BlockSpec(memory_space=pltpu.VMEM)] * count,
        scratch_shapes=[pltpu.SemaphoreType.DMA(s) for s in sems],
        compiler_params=pltpu.CompilerParams(collective_id=collective_id, has_side_effects=True),
        name=f"gather{collective_id}",
    )(*arrays)


def shifted(array, axis, offset):
    devices = lax.axis_size(axis)
    return lax.ppermute(array, axis, [(d, (d + offset) % devices) for d in range(devices)])


def from_owners(array):
    owners = lax.axis_size("expert")
    return jnp.stack([array] + [shifted(array, "expert", e) for e in range(1, owners)])


def to_owners(array):
    owners = lax.axis_size("expert")
    total = array[0].astype(jnp.float32)
    for e in range(1, owners):
        total = total + shifted(array[e], "expert", owners - e).astype(jnp.float32)
    return total


def rounded_up(value, multiple):
    return -(-value // multiple) * multiple


def per_device(
    inputs,
    first_gain,
    first_bias,
    attention_in,
    attention_out,
    second_gain,
    second_bias,
    router_weight,
    expert_in,
    expert_out,
    expert_ids,
    slot_index,
    cotangent,
):
    bf16, f32 = jnp.bfloat16, jnp.float32
    tokens_here = inputs.shape[0]
    model_width = inputs.shape[1]
    images = tokens_here // SEQ
    local_width = attention_in.shape[2]
    local_heads = local_width // HEAD_DIM
    owners = lax.axis_size("expert")
    cuts = lax.axis_size("tensor")
    experts_here = expert_in.shape[0]
    experts_all = experts_here * owners
    capacity = (2 * tokens_here - 1) // experts_all
    scaling = HEAD_DIM ** (-0.5)
    rows = rounded_up(rounded_up(tokens_here, cuts) // cuts, 8)
    padded = rows * cuts
    lanes = rounded_up(experts_all, 128)
    slots = rounded_up(owners * capacity, 16)
    piece = lax.axis_index("tensor")

    def split_heads(matrix):
        return matrix.reshape(images, SEQ, local_heads, HEAD_DIM)

    def pad_rows(matrix, value=0):
        return jnp.pad(
            matrix, ((0, padded - tokens_here), (0, 0)), constant_values=value
        )

    def my_rows(matrix):
        return lax.dynamic_slice_in_dim(pad_rows(matrix), piece * rows, rows, 0)

    target = jnp.where(slot_index < capacity, expert_ids * capacity + slot_index, -1)
    target_all = from_owners(pad_rows(target, -1).astype(f32).T)
    cot_all = from_owners(pad_rows(cotangent)).reshape(owners * padded, model_width)

    x_full = inputs.astype(f32)
    normed1, scale1 = normalize(x_full)
    first = (normed1 * first_gain + first_bias).astype(bf16)
    project = [
        jnp.dot(first, attention_in[which], preferred_element_type=f32).astype(bf16)
        for which in range(3)
    ]
    query_h, keys_h, values_h = [split_heads(part) for part in project]
    scores = jnp.einsum("iqhd,ikhd->ihqk", query_h, keys_h, preferred_element_type=f32) * scaling
    peak = jnp.max(scores, axis=-1, keepdims=True)
    logsum = peak[..., 0] + jnp.log(jnp.sum(jnp.exp(scores - peak), axis=-1))
    probs = jnp.exp(scores - logsum[..., None])
    weights = probs.astype(bf16)
    context_h = jnp.einsum(
        "ihqk,ikhd->iqhd", weights, values_h, preferred_element_type=f32
    ).astype(bf16)
    context = context_h.reshape(tokens_here, local_width)
    partial_attn = jnp.dot(pad_rows(context), attention_out, preferred_element_type=f32)
    (attn_parts,) = scattered([partial_attn.astype(bf16).reshape(cuts, rows, model_width)], 1)

    attended = jnp.sum(attn_parts.astype(f32), axis=0)
    resid = my_rows(inputs).astype(f32) + attended
    normed2, scale2 = normalize(resid)
    second = (normed2 * second_gain + second_bias).astype(bf16)
    logits = jnp.dot(second.astype(f32), router_weight, precision=lax.Precision.HIGHEST)
    route = jax.nn.softmax(logits, axis=-1)
    route_wide = jnp.pad(route, ((0, 0), (0, lanes - experts_all)))
    second_all, route_all = gathered([second, route_wide], 2, forward=True)
    second_all = second_all.reshape(owners * padded, model_width)
    route_all = route_all.reshape(owners * padded, lanes)

    base = lax.axis_index("expert") * experts_here
    block = jnp.arange(owners, dtype=jnp.int32)[:, None, None] * capacity
    place = target_all.astype(jnp.int32)
    local_row = jnp.arange(slots, dtype=jnp.int32)
    first_slot = (base + jnp.arange(experts_here, dtype=jnp.int32)) * capacity
    offset = place[None] - first_slot[:, None, None, None]
    row_of = jnp.where((offset >= 0) & (offset < capacity), offset + block[None], -1)
    picks = row_of[:, None] == local_row[None, :, None, None, None]
    chosen = jnp.any(picks, axis=3).reshape(experts_here, slots, owners * padded)
    placing = chosen.astype(bf16)
    route_here = lax.dynamic_slice_in_dim(route_all, base, experts_here, 1).T
    slot_gate = jnp.sum(jnp.where(chosen, route_here[:, None, :], 0.0), axis=-1)
    received = jnp.einsum("kct,td->kcd", placing, second_all, preferred_element_type=f32).astype(
        bf16
    )
    slotted = jnp.einsum("kct,td->kcd", placing, cot_all, preferred_element_type=f32)
    y_grad = (slot_gate[..., None] * slotted).astype(bf16)
    pre = jnp.einsum("kcd,kdf->kcf", received, expert_in, preferred_element_type=f32)
    value, slope = gelu_parts(pre)
    hidden = value.astype(bf16)
    partial_y = jnp.einsum("kcf,kfd->kcd", hidden, expert_out, preferred_element_type=f32)
    gated_y = (slot_gate[..., None] * partial_y).astype(bf16)
    mixed = jnp.einsum("kct,kcd->td", placing, gated_y, preferred_element_type=f32).astype(bf16)
    mixed_home = to_owners(mixed.reshape(owners, padded, model_width))
    slot_grad = jnp.sum(slotted * partial_y, axis=-1)
    route_part = jnp.sum(jnp.where(chosen, slot_grad[..., None], 0.0), axis=1)
    spot = jnp.arange(lanes, dtype=jnp.int32)[:, None] == base + jnp.arange(
        experts_here, dtype=jnp.int32
    )
    route_part = jnp.sum(
        jnp.where(spot[None], route_part.T[:, None, :], 0.0), axis=-1
    ).reshape(owners, padded, lanes)
    route_home = to_owners(route_part)
    hidden_grad = jnp.einsum("kcd,kfd->kcf", y_grad, expert_out, preferred_element_type=f32)
    pre_grad = (hidden_grad * slope).astype(bf16)
    partial_back = jnp.einsum("kcf,kdf->kcd", pre_grad, expert_in, preferred_element_type=f32)
    back = jnp.einsum(
        "kct,kcd->td", placing, partial_back.astype(bf16), preferred_element_type=f32
    ).astype(bf16)
    back_home = to_owners(back.reshape(owners, padded, model_width))
    local_out_grad = jnp.einsum("kcf,kcd->kfd", hidden, y_grad, preferred_element_type=f32)
    local_in_grad = jnp.einsum("kcd,kcf->kdf", received, pre_grad, preferred_element_type=f32)
    expert_in_grad, expert_out_grad = (
        lax.psum_scatter(
            local_in_grad.astype(bf16), "dp", scatter_dimension=1, tiled=True
        ).astype(f32),
        lax.psum_scatter(
            local_out_grad.astype(bf16), "dp", scatter_dimension=2, tiled=True
        ).astype(f32),
    )
    parts = scattered(
        [
            mixed_home.astype(bf16).reshape(cuts, rows, model_width),
            back_home.astype(bf16).reshape(cuts, rows, model_width),
            route_home.reshape(cuts, rows, lanes),
        ],
        3,
    )
    moe, back_rows, route_grad = [jnp.sum(part.astype(f32), axis=0) for part in parts]
    route_grad = route_grad[:, :experts_all]

    layer_rows = resid + moe
    grad_out = my_rows(cotangent).astype(f32)
    logit_grad = route * (route_grad - jnp.sum(route * route_grad, axis=-1, keepdims=True))
    local_router = jnp.dot(
        second.astype(f32).T, logit_grad, precision=lax.Precision.HIGHEST
    )
    second_grad = back_rows + jnp.dot(logit_grad, router_weight.T, precision=lax.Precision.HIGHEST)
    local_second_gain = jnp.sum(second_grad * normed2, axis=0)
    local_second_bias = jnp.sum(second_grad, axis=0)
    resid_grad = grad_out + norm_back(second_grad, normed2, scale2, second_gain)
    resid_all, layer_all = gathered([resid_grad.astype(bf16), layer_rows.astype(bf16)], 4)
    resid_low = resid_all.reshape(padded, model_width)[:tokens_here]
    layer_out = layer_all.reshape(padded, model_width)[:tokens_here].astype(f32)

    local_attn_out = jnp.einsum("rh,rd->hd", context, resid_low, preferred_element_type=f32)
    context_grad = jnp.einsum(
        "rd,hd->rh", resid_low, attention_out, preferred_element_type=f32
    ).astype(bf16)
    context_g = split_heads(context_grad)
    values_grad = jnp.einsum(
        "ihqk,iqhd->ikhd", weights, context_g, preferred_element_type=f32
    ).astype(bf16)
    probs_grad = jnp.einsum("iqhd,ikhd->ihqk", context_g, values_h, preferred_element_type=f32)
    delta = jnp.transpose(
        jnp.sum(context_g.astype(f32) * context_h.astype(f32), axis=-1), (0, 2, 1)
    )
    score_grad = (probs * (probs_grad - delta[..., None]) * scaling).astype(bf16)
    query_grad = jnp.einsum(
        "ihqk,ikhd->iqhd", score_grad, keys_h, preferred_element_type=f32
    ).astype(bf16)
    keys_grad = jnp.einsum(
        "ihqk,iqhd->ikhd", score_grad, query_h, preferred_element_type=f32
    ).astype(bf16)
    grads_flat = [
        part.reshape(tokens_here, local_width) for part in (query_grad, keys_grad, values_grad)
    ]
    partial_first = sum(
        jnp.einsum("rh,dh->rd", grads_flat[k], attention_in[k], preferred_element_type=f32)
        for k in range(3)
    )
    (first_parts,) = scattered(
        [pad_rows(partial_first).astype(bf16).reshape(cuts, rows, model_width)], 5
    )
    local_attn_in = jnp.stack(
        [
            jnp.einsum("rd,rh->dh", first, part, preferred_element_type=f32)
            for part in grads_flat
        ]
    )
    local_first_gain = jnp.sum(partial_first * normed1, axis=0)
    local_first_bias = jnp.sum(partial_first, axis=0)
    small = jnp.concatenate(
        [
            local_router.T,
            jnp.stack([local_first_gain, local_first_bias, local_second_gain, local_second_bias]),
        ]
    ).astype(bf16)
    small_sum = sent_and_summed(small, ("dp", "expert"), 1)
    attention_in_grad = sent_and_summed(local_attn_in.astype(bf16), ("dp", "expert"), 1)
    attention_out_grad = sent_and_summed(local_attn_out.astype(bf16), ("dp", "expert"), 1)

    first_grad = jnp.sum(first_parts.astype(f32), axis=0)
    normed1_rows, scale1_rows = normalize(my_rows(inputs).astype(f32))
    grad_rows = resid_grad + norm_back(first_grad, normed1_rows, scale1_rows, first_gain)
    tall = rounded_up(small_sum.shape[0], 8)
    wide = rounded_up(small_sum.shape[1], 128)
    small_pad = jnp.pad(
        small_sum, ((0, tall - small_sum.shape[0]), (0, wide - small_sum.shape[1]))
    )
    grad_all, small_all = gathered([grad_rows.astype(bf16), small_pad], 6)
    input_grad = grad_all.reshape(padded, model_width)[:tokens_here].astype(f32)
    totals = jnp.sum(small_all[0], axis=0)[: small_sum.shape[0], : small_sum.shape[1]]
    return (
        layer_out,
        input_grad,
        totals[experts_all],
        totals[experts_all + 1],
        attention_in_grad,
        attention_out_grad,
        totals[experts_all + 2],
        totals[experts_all + 3],
        totals[:experts_all].T,
        expert_in_grad,
        expert_out_grad,
    )


def solution(mesh):
    in_specs = (
        P(("dp", "expert"), None),
        P(),
        P(),
        P(None, None, "tensor"),
        P("tensor", None),
        P(),
        P(),
        P(),
        P("expert", None, "tensor"),
        P("expert", "tensor", None),
        P(("dp", "expert"), None),
        P(("dp", "expert"), None),
        P(("dp", "expert"), None),
    )
    out_specs = (
        P(("dp", "expert"), None),
        P(("dp", "expert"), None),
        P(("dp", "expert")),
        P(("dp", "expert")),
        P(None, ("dp", "expert"), "tensor"),
        P("tensor", ("dp", "expert")),
        P(("dp", "expert")),
        P(("dp", "expert")),
        P(("dp", "expert"), None),
        P("expert", "dp", "tensor"),
        P("expert", "tensor", "dp"),
    )
    return jax.shard_map(
        per_device, mesh=mesh, in_specs=in_specs, out_specs=out_specs, check_vma=False
    )
```

time: 341 us -> 247 us (0.72)
  waiting for transfers between devices: 153 us -> 15.8 us
  Pallas kernels: 0 us -> 93.9 us
  blocking collectives: 47.3 us -> 0 us
  other arithmetic: 21 us -> 42.3 us
  starting transfers between devices: 29.3 us -> 17.7 us
  local copies, waits for them, and re-layouts: 36.2 us -> 27.4 us
  matrix products: 37.3 us -> 32.9 us
    pallas_call x0 -> x6, Pallas kernels: none -> 93.9 us  [the longest x3 51.3 us: gathered(): pl.pallas_call(functools.partial(gather_kernel, count, forward), out_shap...]
    psum x3 -> x0, waiting for transfers between devices: 81.7 us -> none  [the longest x1 42.5 us: per_device(): attended = lax.psum(partial_attn, 'tensor')]
    psum x1 -> x0, blocking collectives: 47.3 us -> none  [per_device(): summed = lax.psum(partial_value, 'tensor')]
    reduce_scatter x2, waiting for transfers between devices: 37.6 us -> 0.01 us  [the longest x1 0.01 us: per_device(): lax.psum_scatter(local_in_grad.astype(bf16), 'dp', scatter_dimension=1, t...]
    all_to_all x4 -> x0, starting transfers between devices: 17 us -> none  [the longest x1 4.26 us: per_device(): lax.all_to_all(grad_send, 'expert', split_axis=0, concat_axis=0, tiled=True)]
    reshape x7 -> x0, local copies, waits for them, and re-layouts: 13.5 us -> none  [the longest x2 4.43 us: per_device(): sendbuf = sendbuf.reshape(owners, experts_here, capacity, model_width)]
    all_to_all x3, waiting for transfers between devices: 25.3 us -> 12.6 us  [sent_and_summed(): lax.all_to_all(cut_along(shard, dim, devices), axis, 0, 0, tiled=True)]
    convert_element_type x2 -> x8, other arithmetic: 2.01 us -> 10.4 us  [the longest x1 1.89 us: per_device(): mixed_home.astype(bf16).reshape(cuts, rows, model_width)]
  transfers between devices with their start and end apart: 12 -> 10, of which waited for: 9 -> 2; matrix products, arithmetic and copies ran while one was open for 18% -> 35% of each run, Pallas kernels for 0% -> 38%
where the time goes in v1:
time: 247 us; the launch traced here: 245 us
  Pallas kernels  93.9 us (38%)
  other arithmetic  42.3 us (17%)
  matrix products  32.9 us (13%)
  local copies, waits for them, and re-layouts  27.4 us (11%)
  starting transfers between devices  17.7 us (7%)
  waiting for transfers between devices  15.8 us (6%)
  between operations  14.9 us (6%)
    pallas_call x3, Pallas kernels, gathered(): pl.pallas_call(functools.partial(gather_kernel, count, forward), out_shap...  51.3 us
    pallas_call x3, Pallas kernels, scattered(): pl.pallas_call(functools.partial(scatter_kernel, count), out_shape=[jax.S...  42.5 us
    all_to_all x3, waiting for transfers between devices, sent_and_summed(): lax.all_to_all(cut_along(shard, dim, devices), axis, 0, 0, tiled=True)  12.6 us
    all_to_all x3, starting transfers between devices, sent_and_summed(): lax.all_to_all(cut_along(shard, dim, devices), axis, 0, 0, tiled=True)  11.7 us
    unnamed x104, local copies, waits for them, and re-layouts  7.25 us
    ppermute x5, starting transfers between devices, shifted(): lax.ppermute(array, axis, [(d, (d + offset) % devices) for d in range(dev...  5.71 us
  transfers between devices with their start and end apart: 10, of which 2 were waited for; matrix products, arithmetic and copies ran while one was open for 35% of the time, Pallas kernels for 38%

profile of v1, /device:TPU:0, one launch (start us, length us, event | category | flops | bytes accessed | tf_op | source)
XLA Modules:
  0.0 245.0 jit_solution(4526609646662731811)
XLA Ops:
  8.7 3.0 %collective-permute-start = (f32[2,224]{1,0:T(2,128)}, f32[2,224]{1,0:T(2,128)}, u32[]{:S(2)}, u32[]{:S(2)}) collective-permute-start(f32[2,224]{1,0:T(2,128)} %get-tuple-element.54), channel_id=1, source_target_pairs={{0,4},{4,0},{1,5},{5,1},{2,6},{6,2},{3,7},{7,3},{8,12},{12,8},{9,1... | collective-permute-start | bytes 5384 | tf_op jit(solution)/shard_map/ppermute | solution.py:196
  11.7 1.9 pad_bitcast_fusion
  18.2 11.9 %scatter1.1 = bf16[4,56,768]{2,1,0:T(8,128)(2,1)} custom-call(bf16[4,56,768]{2,1,0:T(8,128)(2,1)} %bitcast.169), custom_call_target="tpu_custom_call" | custom-call | tf_op jit(solution)/shard_map/scatter1/pallas_call | solution.py:111
  36.3 2.0 fusion.69
  43.2 19.9 %gather2.1 = (bf16[2,4,56,768]{3,2,1,0:T(8,128)(2,1)}, f32[2,4,56,128]{3,2,1,0:T(8,128)}) custom-call(bf16[56,768]{1,0:T(8,128)(2,1)} %copy-done.7, f32[56,128]{1,0:T(8,128)} %pad.34.refs_1_), custom_call_target="tpu_custom_call" | custom-call | tf_op jit(solution)/shard_map/gather2/pallas_call | solution.py:181
  79.2 2.2 convolution_convert_fusion.1
  83.5 2.0 fusion.1
  92.7 4.0 %convolution_convert_fusion = bf16[2,768,768]{1,2,0:T(8,128)(2,1)} fusion(f32[2,208,768]{2,1,0:T(8,128)} %copy-done.4, f32[2,208]{1,0:T(2,128)} %copy-done.32, f32[2,208,768]{2,1,0:T(8,128)} %copy-done.3), kind=kOutput, calls=%fused_computation.1 | convolution fusion | flops 495427584 | bytes 4916864 | tf_op jit(solution)/shard_map/kcf,kcd->kfd/dot_general | solution.py:335
  96.7 3.3 %fusion.2 = bf16[448,768]{1,0:T(8,128)(2,1)} fusion(pred[2,208,448]{1,2,0:T(32,128)(4,1)} %bitcast.172, bf16[2,208,768]{2,1,0:T(8,128)(2,1)} %copy-done.17, bf16[2,768,768]{2,1,0:T(8,128)(2,1)S(1)} %copy-done), kind=kOutput, calls=%fused_computation.12 | convolution fusion | flops 777658368 | bytes 3872768 | tf_op jit(solution)/shard_map/kct,kcd->td/dot_general | solution.py:331
  104.2 1.9 add_convert_fusion.1
  106.1 3.2 %collective-permute-done.3 = bf16[224,768]{1,0:T(8,128)(2,1)} collective-permute-done((bf16[224,768]{1,0:T(8,128)(2,1)}, bf16[224,768]{1,0:T(8,128)(2,1)}, u32[]{:S(2)}, u32[]{:S(2)}) %collective-permute-start.3) | collective-permute-done | bytes 344096 | tf_op jit(solution)/shard_map/ppermute | solution.py:196
  111.1 18.0 %scatter3.1 = (bf16[4,56,768]{2,1,0:T(8,128)(2,1)}, bf16[4,56,768]{2,1,0:T(8,128)(2,1)}, f32[4,56,128]{2,1,0:T(8,128)}) custom-call(bf16[4,56,768]{2,1,0:T(8,128)(2,1)} %bitcast.166, bf16[4,56,768]{2,1,0:T(8,128)(2,1)} %bitcast.167, f32[4,56,128]{2,1,0:T(8,128)} %bitcast.181), custom_call_target="tpu_custom_call" | custom-call | tf_op jit(solution)/shard_map/scatter3/pallas_call | solution.py:111
  135.1 2.6 %multiply_reduce_fusion.1 = (bf16[768]{0:T(1024)(128)(2,1)}, f32[56]{0:T(128)S(1)}, f32[56]{0:T(128)S(1)}, bf16[768]{0:T(1024)(128)(2,1)}, bf16[56,768]{1,0:T(8,128)(2,1)}, /*index=5*/f32[56,768]{1,0:T(8,128)S(1)}) fusion(f32[56,768]{1,0:T(8,128)S(1)} %get-tuple-element.42, f32[56]{0:T(128)} %add_rsqrt_fusion.2, f32[56]{0:T(128)} %copy-done.36, ...), kind=kOutput, calls=%fused_computation.112 | convolution fusion | flops 2579280 | bytes 823264 | tf_op jit(solution)/shard_map/dot_general | solution.py:362
  139.4 19.2 %gather4.1 = (bf16[1,4,56,768]{3,2,1,0:T(8,128)(2,1)}, bf16[1,4,56,768]{3,2,1,0:T(8,128)(2,1)}) custom-call(bf16[56,768]{1,0:T(8,128)(2,1)} %get-tuple-element.39.refs_0_, bf16[56,768]{1,0:T(8,128)(2,1)} %get-tuple-element.48.refs_1_), custom_call_target="tpu_custom_call" | custom-call | tf_op jit(solution)/shard_map/gather4/pallas_call | solution.py:181
  164.7 12.7 %scatter5.1 = bf16[4,56,768]{2,1,0:T(8,128)(2,1)} custom-call(bf16[4,56,768]{2,1,0:T(8,128)(2,1)} %bitcast.168), custom_call_target="tpu_custom_call" | custom-call | tf_op jit(solution)/shard_map/scatter5/pallas_call | solution.py:111
  178.8 3.3 %all-to-all-start = ((bf16[8,8,96]{2,1,0:T(8,128)(2,1)}), bf16[8,8,96]{2,1,0:T(8,128)(2,1)S(1)}, u32[]{:S(2)}, u32[]{:S(2)}) async-start(bf16[8,8,96]{2,1,0:T(8,128)(2,1)} %bitcast.48), calls=%async_computation | async-start | bytes 32768 | tf_op jit(solution)/shard_map/all_to_all | solution.py:27
  192.6 4.1 %all-to-all-start.2 = ((bf16[8,192,96]{2,1,0:T(8,128)(2,1)}), bf16[8,192,96]{2,1,0:T(8,128)(2,1)S(1)}, u32[]{:S(2)}, u32[]{:S(2)}) async-start(bf16[8,192,96]{2,1,0:T(8,128)(2,1)} %bitcast.160), calls=%async_computation.2 | async-start | bytes 786432 | tf_op jit(solution)/shard_map/all_to_all | solution.py:27
  198.1 12.2 %gather6.1 = (bf16[1,4,56,768]{3,2,1,0:T(8,128)(2,1)}, f32[1,4,8,128]{3,2,1,0:T(8,128)}) custom-call(bf16[56,768]{1,0:T(8,128)(2,1)} %fusion.51.refs_0_, f32[8,128]{1,0:T(8,128)} %pad.36.refs_1_), custom_call_target="tpu_custom_call" | custom-call | tf_op jit(solution)/shard_map/gather6/pallas_call | solution.py:181
  211.1 4.3 %all-to-all-start.1 = ((bf16[8,3,96,192]{3,2,1,0:T(8,128)(2,1)}), bf16[8,3,96,192]{3,2,1,0:T(8,128)(2,1)}, u32[]{:S(2)}, u32[]{:S(2)}) async-start(bf16[8,3,96,192]{3,2,1,0:T(8,128)(2,1)} %copy.109), calls=%async_computation.1 | async-start | bytes 2359296 | tf_op jit(solution)/shard_map/all_to_all | solution.py:27
  216.5 1.8 slice_convert_fusion
  219.0 12.6 %all-to-all-done.1 = bf16[8,3,96,192]{3,2,1,0:T(8,128)(2,1)} async-done(((bf16[8,3,96,192]{3,2,1,0:T(8,128)(2,1)}), bf16[8,3,96,192]{3,2,1,0:T(8,128)(2,1)}, u32[]{:S(2)}, u32[]{:S(2)}) %all-to-all-start.1) | async-done | bytes 884768 | tf_op jit(solution)/shard_map/all_to_all | solution.py:27
  231.6 2.2 convert_reduce_fusion
  233.8 2.2 convert_element_type.273
  236.0 2.2 convert_element_type.275
  (215 shorter events, 77.5 us)
Async XLA Ops:
  7.2 64.3 %copy-start = (bf16[2,768,768]{2,1,0:T(8,128)(2,1)S(1)}, bf16[2,768,768]{2,1,0:T(8,128)(2,1)}, u32[]{:S(2)}) copy-start(bf16[2,768,768]{2,1,0:T(8,128)(2,1)} %param.21) | copy-start | bytes 7077892
  7.2 7.5 %copy-start.1 = (bf16[197,768]{1,0:T(8,128)(2,1)S(1)}, bf16[197,768]{1,0:T(8,128)(2,1)}, u32[]{:S(2)}) copy-start(bf16[197,768]{1,0:T(8,128)(2,1)} %param.13) | copy-start | bytes 907780
  7.2 7.7 %copy-start.50 = (f32[768]{0:T(1024)S(1)}, f32[768]{0:T(1024)}, u32[]{:S(2)}) copy-start(f32[768]{0:T(1024)} %param.15) | copy-start | bytes 9220
  7.2 7.7 %copy-start.33 = (f32[768]{0:T(1024)S(1)}, f32[768]{0:T(1024)}, u32[]{:S(2)}) copy-start(f32[768]{0:T(1024)} %param.14) | copy-start | bytes 9220
  7.2 226.6 %reduce-scatter.3.cloned.1.call-start = ((), (), s32[]{:S(2)}) async-start(), calls=%async_computation.5 | async-start | bytes 2949120 | tf_op jit(solution)/shard_map/reduce_scatter | solution.py:338
  7.3 7.7 %copy-start.23 = (bf16[3,768,192]{1,2,0:T(8,128)(2,1)S(1)}, bf16[3,768,192]{1,2,0:T(8,128)(2,1)}, u32[]{:S(2)}) copy-start(bf16[3,768,192]{1,2,0:T(8,128)(2,1)} %param.16) | copy-start | bytes 2654212
  8.7 58.3 %collective-permute-start = (f32[2,224]{1,0:T(2,128)}, f32[2,224]{1,0:T(2,128)}, u32[]{:S(2)}, u32[]{:S(2)}) collective-permute-start(f32[2,224]{1,0:T(2,128)} %get-tuple-element.54), channel_id=1, source_target_pairs={{0,4},{4,0},{1,5},{5,1},{2,6},{6,2},{3,7},{7,3},{8,12},{12,8},{9,1... | collective-permute-start | bytes 5384 | tf_op jit(solution)/shard_map/ppermute | solution.py:196
  13.6 60.4 %collective-permute-start.2 = (bf16[224,768]{1,0:T(8,128)(2,1)}, bf16[224,768]{1,0:T(8,128)(2,1)}, u32[]{:S(2)}, u32[]{:S(2)}) collective-permute-start(bf16[224,768]{1,0:T(8,128)(2,1)} %get-tuple-element.47), channel_id=1, source_target_pairs={{0,4},{4,0},{1,5},{5,1},{2,6},{6,2},{3,7},{7,3},{8,12},{12,8},{9,1... | collective-permute-start | bytes 1032200 | tf_op jit(solution)/shard_map/ppermute | solution.py:196
  81.5 154.5 %reduce-scatter.5.cloned.1.call-start = ((), (), s32[]{:S(2)}) async-start(), calls=%async_computation.6 | async-start | bytes 2949120 | tf_op jit(solution)/shard_map/reduce_scatter | solution.py:341
  87.0 17.2 %collective-permute-start.1 = (bf16[224,768]{1,0:T(8,128)(2,1)}, bf16[224,768]{1,0:T(8,128)(2,1)}, u32[]{:S(2)}, u32[]{:S(2)}) collective-permute-start(bf16[224,768]{1,0:T(8,128)(2,1)} %slice.88), channel_id=1, source_target_pairs={{0,4},{4,0},{1,5},{5,1},{2,6},{6,2},{3,7},{7,3},{8,12},{12,8},{9,1... | collective-permute-start | bytes 1032200 | tf_op jit(solution)/shard_map/ppermute | solution.py:196
  91.2 11.3 %collective-permute-start.4 = (f32[224,128]{1,0:T(8,128)}, f32[224,128]{1,0:T(8,128)}, u32[]{:S(2)}, u32[]{:S(2)}) collective-permute-start(f32[224,128]{1,0:T(8,128)} %slice.92), channel_id=1, source_target_pairs={{0,4},{4,0},{1,5},{5,1},{2,6},{6,2},{3,7},{7,3},{8,12},{12,8},{9,1... | collective-permute-start | bytes 344072 | tf_op jit(solution)/shard_map/ppermute | solution.py:196
  101.7 7.6 %collective-permute-start.3 = (bf16[224,768]{1,0:T(8,128)(2,1)}, bf16[224,768]{1,0:T(8,128)(2,1)}, u32[]{:S(2)}, u32[]{:S(2)}) collective-permute-start(bf16[224,768]{1,0:T(8,128)(2,1)} %slice.90), channel_id=1, source_target_pairs={{0,4},{4,0},{1,5},{5,1},{2,6},{6,2},{3,7},{7,3},{8,12},{12,8},{9,1... | collective-permute-start | bytes 1032200 | tf_op jit(solution)/shard_map/ppermute | solution.py:196
  102.5 6.8 %copy-start.16 = (bf16[448,768]{1,0:T(8,128)(2,1)S(1)}, bf16[448,768]{1,0:T(8,128)(2,1)}, u32[]{:S(2)}) copy-start(bf16[448,768]{1,0:T(8,128)(2,1)} %fusion.2) | copy-start | bytes 2064388
  139.4 21.9 %copy-start.28 = (bf16[197,192]{0,1:T(8,128)(2,1)S(1)}, bf16[197,192]{0,1:T(8,128)(2,1)}, u32[]{:S(2)}) copy-start(bf16[197,192]{0,1:T(8,128)(2,1)} %copy-done.27) | copy-start | bytes 226948
  162.8 14.5 %copy-start.8 = (bf16[56,768]{1,0:T(8,128)(2,1)S(1)}, bf16[56,768]{1,0:T(8,128)(2,1)}, u32[]{:S(2)}) copy-start(bf16[56,768]{1,0:T(8,128)(2,1)} %copy-done.7) | copy-start | bytes 258052
  162.8 14.5 %copy-start.19 = (f32[56,4]{1,0:T(8,128)S(1)}, f32[56,4]{1,0:T(8,128)}, u32[]{:S(2)}) copy-start(f32[56,4]{1,0:T(8,128)} %copy-done.18) | copy-start | bytes 2692
  162.8 14.5 %copy-start.20 = (f32[56,128]{1,0:T(8,128)S(1)}, f32[56,128]{1,0:T(8,128)}, u32[]{:S(2)}) copy-start(f32[56,128]{1,0:T(8,128)} %reduce_sum.296) | copy-start | bytes 86020
  162.9 14.5 %copy-start.42 = (f32[56]{0:T(128)S(1)}, f32[56]{0:T(128)}, u32[]{:S(2)}) copy-start(f32[56]{0:T(128)} %copy-done.41) | copy-start | bytes 676
  163.9 14.0 %copy-start.38 = (bf16[768]{0:T(1024)(128)(2,1)S(1)}, bf16[768]{0:T(1024)(128)(2,1)}, u32[]{:S(2)}) copy-start(bf16[768]{0:T(1024)(128)(2,1)} %get-tuple-element.31) | copy-start | bytes 4612
  163.9 14.1 %copy-start.37 = (bf16[768]{0:T(1024)(128)(2,1)S(1)}, bf16[768]{0:T(1024)(128)(2,1)}, u32[]{:S(2)}) copy-start(bf16[768]{0:T(1024)(128)(2,1)} %get-tuple-element.38) | copy-start | bytes 4612
  163.9 20.5 %copy-start.40 = (f32[56]{0:T(128)S(1)}, f32[56]{0:T(128)}, u32[]{:S(2)}) copy-start(f32[56]{0:T(128)} %copy-done.39) | copy-start | bytes 676
  178.8 13.8 %all-to-all-start = ((bf16[8,8,96]{2,1,0:T(8,128)(2,1)}), bf16[8,8,96]{2,1,0:T(8,128)(2,1)S(1)}, u32[]{:S(2)}, u32[]{:S(2)}) async-start(bf16[8,8,96]{2,1,0:T(8,128)(2,1)} %bitcast.48), calls=%async_computation | async-start | bytes 32768 | tf_op jit(solution)/shard_map/all_to_all | solution.py:27
  192.6 18.5 %all-to-all-start.2 = ((bf16[8,192,96]{2,1,0:T(8,128)(2,1)}), bf16[8,192,96]{2,1,0:T(8,128)(2,1)S(1)}, u32[]{:S(2)}, u32[]{:S(2)}) async-start(bf16[8,192,96]{2,1,0:T(8,128)(2,1)} %bitcast.160), calls=%async_computation.2 | async-start | bytes 786432 | tf_op jit(solution)/shard_map/all_to_all | solution.py:27
  211.1 20.5 %all-to-all-start.1 = ((bf16[8,3,96,192]{3,2,1,0:T(8,128)(2,1)}), bf16[8,3,96,192]{3,2,1,0:T(8,128)(2,1)}, u32[]{:S(2)}, u32[]{:S(2)}) async-start(bf16[8,3,96,192]{3,2,1,0:T(8,128)(2,1)} %copy.109), calls=%async_computation.1 | async-start | bytes 2359296 | tf_op jit(solution)/shard_map/all_to_all | solution.py:27
  (38 other events, 68.0 us)
Sparse Core Ops, SparseCore 0:
  81.6 33.6 reduce-scatter.2
  117.8 32.8 reduce-scatter.4

commit v2 on v1

--- a/solution.py
+++ b/solution.py
@@ -77,6 +77,92 @@
             pl.semaphore_signal(barrier, inc=1, device_id={axis: peer}, device_id_type=MESH)
             peers += 1
     pl.semaphore_wait(barrier, peers)
+
+
+def group_peer(k):
+    owners = lax.axis_size("expert")
+    members = lax.axis_size("dp") * owners
+    me = lax.axis_index("dp") * owners + lax.axis_index("expert")
+    peer = lax.rem(me + k, members)
+    return {"dp": peer // owners, "expert": lax.rem(peer, owners)}
+
+
+def greet_line_and_group(grouped):
+    barrier = pltpu.get_barrier_semaphore()
+    cuts = lax.axis_size("tensor")
+    members = lax.axis_size("dp") * lax.axis_size("expert") if grouped else 1
+    for k in range(1, cuts):
+        peer = {"tensor": lax.rem(lax.axis_index("tensor") + k, cuts)}
+        pl.semaphore_signal(barrier, inc=1, device_id=peer, device_id_type=MESH)
+    for k in range(1, members):
+        pl.semaphore_signal(barrier, inc=1, device_id=group_peer(k), device_id_type=MESH)
+    pl.semaphore_wait(barrier, cuts + members - 2)
+
+
+def group_copies(source, target, send_sem, recv_sem):
+    owners = lax.axis_size("expert")
+    members = lax.axis_size("dp") * owners
+    me = lax.axis_index("dp") * owners + lax.axis_index("expert")
+    copies = []
+    for k in range(1, members):
+        copy = pltpu.make_async_remote_copy(
+            src_ref=source.at[lax.rem(me + k, members)],
+            dst_ref=target.at[k],
+            send_sem=send_sem.at[k],
+            recv_sem=recv_sem.at[k],
+            device_id=group_peer(k),
+            device_id_type=MESH,
+        )
+        copy.start()
+        copies.append(copy)
+    target[0] = source[me]
+    return copies
+
+
+def ends_kernel(gather, *refs):
+    source, group_source, target, group_target = refs[:4]
+    send_sem, recv_sem, send_group, recv_group = refs[4:]
+    devices = lax.axis_size("tensor")
+    me = lax.axis_index("tensor")
+    greet_line_and_group(True)
+    copies = []
+    for k in range(1, devices):
+        peer = lax.rem(me + k, devices)
+        copy = pltpu.make_async_remote_copy(
+            src_ref=source if gather else source.at[peer],
+            dst_ref=target.at[me] if gather else target.at[k],
+            send_sem=send_sem.at[k],
+            recv_sem=recv_sem.at[k],
+            device_id={"tensor": peer},
+            device_id_type=MESH,
+        )
+        copy.start()
+        copies.append(copy)
+    copies += group_copies(group_source, group_target, send_group, recv_group)
+    if gather:
+        target[me] = source[...]
+    else:
+        target[0] = source[me]
+    for copy in copies:
+        copy.wait()
+
+
+def line_and_group(array, group_array, collective_id, gather):
+    devices = lax.axis_size("tensor")
+    members = group_array.shape[0]
+    shape = (devices, *array.shape) if gather else array.shape
+    return pl.pallas_call(
+        functools.partial(ends_kernel, gather),
+        out_shape=[
+            jax.ShapeDtypeStruct(shape, array.dtype),
+            jax.ShapeDtypeStruct(group_array.shape, group_array.dtype),
+        ],
+        in_specs=[pl.BlockSpec(memory_space=pltpu.VMEM)] * 2,
+        out_specs=[pl.BlockSpec(memory_space=pltpu.VMEM)] * 2,
+        scratch_shapes=[pltpu.SemaphoreType.DMA((n,)) for n in (devices, devices, members, members)],
+        compiler_params=pltpu.CompilerParams(collective_id=collective_id, has_side_effects=True),
+        name=f"ends{collective_id}",
+    )(array, group_array)
 
 
 def scatter_kernel(count, *refs):
@@ -211,6 +297,117 @@
 
 def rounded_up(value, multiple):
     return -(-value // multiple) * multiple
+
+
+def experts_kernel(
+    experts_all,
+    slot_ref,
+    spot_ref,
+    second_ref,
+    cot_ref,
+    router_ref,
+    in_ref,
+    out_ref,
+    mixed_ref,
+    back_ref,
+    share_ref,
+    route_ref,
+    cut_ref,
+    placing_ref,
+    gated_ref,
+    low_ref,
+    grad_ref,
+):
+    bf16, f32 = jnp.bfloat16, jnp.float32
+    exact = lax.Precision.HIGHEST
+    owners, padded, _ = second_ref.shape
+    experts_here = in_ref.shape[0]
+    lanes = router_ref.shape[1]
+    depth = placing_ref.shape[2]
+
+    def dot(a, b, a_dim, b_dim, precision=None):
+        return lax.dot_general(
+            a, b, (((a_dim,), (b_dim,)), ((), ())), precision=precision, preferred_element_type=f32
+        )
+
+    column = lax.broadcasted_iota(jnp.int32, (padded, lanes), 1)
+    for o in range(owners):
+        logits = dot(second_ref[o].astype(f32), router_ref[...], 1, 0, exact)
+        logits = jnp.where(column < experts_all, logits, -1e30)
+        lifted = jnp.exp(logits - jnp.max(logits, axis=-1, keepdims=True))
+        lifted = jnp.where(column < experts_all, lifted, 0.0)
+        route_ref[o] = lifted / jnp.sum(lifted, axis=-1, keepdims=True)
+    slot = lax.broadcasted_iota(jnp.int32, (depth, padded), 0)
+    for k in range(experts_here):
+        gates, received, slotted = [], [], []
+        for o in range(owners):
+            picks = slot == slot_ref[k, o][None, :]
+            placing = jnp.where(picks, 1.0, 0.0)
+            low = placing.astype(bf16)
+            placing_ref[k, o] = low
+            chances = dot(placing, route_ref[o], 1, 0, exact)
+            gates.append(jnp.sum(chances * spot_ref[k][None, :], axis=-1, keepdims=True))
+            received.append(dot(low, second_ref[o], 1, 0).astype(bf16))
+            slotted.append(dot(low, cot_ref[o], 1, 0))
+        gate = jnp.concatenate(gates)
+        received = jnp.concatenate(received)
+        slotted = jnp.concatenate(slotted)
+        y_grad = (gate * slotted).astype(bf16)
+        value, slope = gelu_parts(dot(received, in_ref[k], 1, 0))
+        hidden = value.astype(bf16)
+        partial_y = dot(hidden, out_ref[k], 1, 0)
+        gated_ref[k] = (gate * partial_y).astype(bf16)
+        slot_grad = jnp.sum(slotted * partial_y, axis=-1, keepdims=True)
+        grad_ref[k] = slot_grad * spot_ref[k][None, :]
+        pre_grad = (dot(y_grad, out_ref[k], 1, 1) * slope).astype(bf16)
+        low_ref[k] = dot(pre_grad, in_ref[k], 1, 1).astype(bf16)
+        in_grad = dot(received, pre_grad, 0, 0).astype(bf16)
+        out_grad = dot(y_grad, hidden, 0, 0).astype(bf16)
+        blocks, _, _, share, _ = cut_ref.shape
+        for d in range(blocks):
+            cut_ref[d, 0, k] = in_grad[d * share : (d + 1) * share]
+            cut_ref[d, 1, k] = out_grad[d * share : (d + 1) * share]
+    for o in range(owners):
+        span = pl.ds(o * depth, depth)
+        here = range(experts_here)
+        mixed_ref[o] = sum(
+            dot(placing_ref[k, o], gated_ref[k, span], 0, 0) for k in here
+        ).astype(bf16)
+        back_ref[o] = sum(dot(placing_ref[k, o], low_ref[k, span], 0, 0) for k in here).astype(bf16)
+        share_ref[o] = sum(
+            dot(placing_ref[k, o].astype(f32), grad_ref[k, span], 0, 0, exact) for k in here
+        )
+
+
+def experts_block(slots, spot, second, cot, router, expert_in, expert_out, experts_all, depth):
+    owners, padded, width = second.shape
+    here, _, hidden = expert_in.shape
+    lanes = router.shape[1]
+    blocks = lax.axis_size("dp")
+    bf16, f32 = jnp.bfloat16, jnp.float32
+    shapes = [
+        ((owners, padded, width), bf16),
+        ((owners, padded, width), bf16),
+        ((owners, padded, lanes), f32),
+        ((owners, padded, lanes), f32),
+        ((blocks, 2, here, width // blocks, hidden), bf16),
+    ]
+    return pl.pallas_call(
+        functools.partial(experts_kernel, experts_all),
+        out_shape=[jax.ShapeDtypeStruct(*s) for s in shapes],
+        in_specs=[pl.BlockSpec(memory_space=pltpu.VMEM)] * 7,
+        out_specs=[pl.BlockSpec(memory_space=pltpu.VMEM)] * 5,
+        scratch_shapes=[
+            pltpu.VMEM((here, owners, depth, padded), bf16),
+            pltpu.VMEM((here, owners * depth, width), bf16),
+            pltpu.VMEM((here, owners * depth, width), bf16),
+            pltpu.VMEM((here, owners * depth, lanes), f32),
+        ],
+        compiler_params=pltpu.CompilerParams(
+            vmem_limit_bytes=(32 << 20) if owners <= 2 else (60 << 20)
+        ),
+        name="experts",
+    )(slots, spot, second, cot, router, expert_in, expert_out)
 
 
 def per_device(
@@ -243,7 +440,6 @@
     rows = rounded_up(rounded_up(tokens_here, cuts) // cuts, 8)
     padded = rows * cuts
     lanes = rounded_up(experts_all, 128)
-    slots = rounded_up(owners * capacity, 16)
     piece = lax.axis_index("tensor")
 
     def split_heads(matrix):
@@ -259,7 +455,7 @@
 
     target = jnp.where(slot_index < capacity, expert_ids * capacity + slot_index, -1)
     target_all = from_owners(pad_rows(target, -1).astype(f32).T)
-    cot_all = from_owners(pad_rows(cotangent)).reshape(owners * padded, model_width)
+    cot_all = from_owners(pad_rows(cotangent))
 
     x_full = inputs.astype(f32)
     normed1, scale1 = normalize(x_full)
@@ -285,63 +481,33 @@
     resid = my_rows(inputs).astype(f32) + attended
     normed2, scale2 = normalize(resid)
     second = (normed2 * second_gain + second_bias).astype(bf16)
-    logits = jnp.dot(second.astype(f32), router_weight, precision=lax.Precision.HIGHEST)
-    route = jax.nn.softmax(logits, axis=-1)
-    route_wide = jnp.pad(route, ((0, 0), (0, lanes - experts_all)))
-    second_all, route_all = gathered([second, route_wide], 2, forward=True)
-    second_all = second_all.reshape(owners * padded, model_width)
-    route_all = route_all.reshape(owners * padded, lanes)
+    (second_all,) = gathered([second], 2, forward=True)
 
     base = lax.axis_index("expert") * experts_here
-    block = jnp.arange(owners, dtype=jnp.int32)[:, None, None] * capacity
-    place = target_all.astype(jnp.int32)
-    local_row = jnp.arange(slots, dtype=jnp.int32)
-    first_slot = (base + jnp.arange(experts_here, dtype=jnp.int32)) * capacity
-    offset = place[None] - first_slot[:, None, None, None]
-    row_of = jnp.where((offset >= 0) & (offset < capacity), offset + block[None], -1)
-    picks = row_of[:, None] == local_row[None, :, None, None, None]
-    chosen = jnp.any(picks, axis=3).reshape(experts_here, slots, owners * padded)
-    placing = chosen.astype(bf16)
-    route_here = lax.dynamic_slice_in_dim(route_all, base, experts_here, 1).T
-    slot_gate = jnp.sum(jnp.where(chosen, route_here[:, None, :], 0.0), axis=-1)
-    received = jnp.einsum("kct,td->kcd", placing, second_all, preferred_element_type=f32).astype(
-        bf16
-    )
-    slotted = jnp.einsum("kct,td->kcd", placing, cot_all, preferred_element_type=f32)
-    y_grad = (slot_gate[..., None] * slotted).astype(bf16)
-    pre = jnp.einsum("kcd,kdf->kcf", received, expert_in, preferred_element_type=f32)
-    value, slope = gelu_parts(pre)
-    hidden = value.astype(bf16)
-    partial_y = jnp.einsum("kcf,kfd->kcd", hidden, expert_out, preferred_element_type=f32)
-    gated_y = (slot_gate[..., None] * partial_y).astype(bf16)
-    mixed = jnp.einsum("kct,kcd->td", placing, gated_y, preferred_element_type=f32).astype(bf16)
-    mixed_home = to_owners(mixed.reshape(owners, padded, model_width))
-    slot_grad = jnp.sum(slotted * partial_y, axis=-1)
-    route_part = jnp.sum(jnp.where(chosen, slot_grad[..., None], 0.0), axis=1)
-    spot = jnp.arange(lanes, dtype=jnp.int32)[:, None] == base + jnp.arange(
-        experts_here, dtype=jnp.int32
-    )
-    route_part = jnp.sum(
-        jnp.where(spot[None], route_part.T[:, None, :], 0.0), axis=-1
-    ).reshape(owners, padded, lanes)
-    route_home = to_owners(route_part)
-    hidden_grad = jnp.einsum("kcd,kfd->kcf", y_grad, expert_out, preferred_element_type=f32)
-    pre_grad = (hidden_grad * slope).astype(bf16)
-    partial_back = jnp.einsum("kcf,kdf->kcd", pre_grad, expert_in, preferred_element_type=f32)
-    back = jnp.einsum(
-        "kct,kcd->td", placing, partial_back.astype(bf16), preferred_element_type=f32
-    ).astype(bf16)
-    back_home = to_owners(back.reshape(owners, padded, model_width))
-    local_out_grad = jnp.einsum("kcf,kcd->kfd", hidden, y_grad, preferred_element_type=f32)
-    local_in_grad = jnp.einsum("kcd,kcf->kdf", received, pre_grad, preferred_element_type=f32)
-    expert_in_grad, expert_out_grad = (
-        lax.psum_scatter(
-            local_in_grad.astype(bf16), "dp", scatter_dimension=1, tiled=True
-        ).astype(f32),
-        lax.psum_scatter(
-            local_out_grad.astype(bf16), "dp", scatter_dimension=2, tiled=True
-        ).astype(f32),
-    )
+    experts = base + jnp.arange(experts_here, dtype=jnp.int32)
+    offset = target_all.astype(jnp.int32)[None] - (experts * capacity)[:, None, None, None]
+    slots = jnp.max(jnp.where((offset >= 0) & (offset < capacity), offset, -1), axis=2)
+    spot = (experts[:, None] == jnp.arange(lanes, dtype=jnp.int32)).astype(f32)
+    mixed, back, share, route_all, expert_cuts = experts_block(
+        slots,
+        spot,
+        second_all.reshape(owners, padded, model_width),
+        cot_all,
+        jnp.pad(router_weight, ((0, 0), (0, lanes - experts_all))),
+        expert_in,
+        expert_out,
+        experts_all,
+        rounded_up(capacity, 16),
+    )
+    route = lax.dynamic_slice_in_dim(route_all[0], piece * rows, rows, 0)[:, :experts_all]
+    mixed_home = to_owners(mixed)
+    back_home = to_owners(back)
+    route_home = to_owners(share)
+    expert_sums = jnp.sum(
+        lax.all_to_all(expert_cuts, "dp", 0, 0, tiled=True).astype(f32), axis=0
+    )
+    expert_in_grad = expert_sums[0]
+    expert_out_grad = jnp.swapaxes(expert_sums[1], 1, 2)
     parts = scattered(
         [
             mixed_home.astype(bf16).reshape(cuts, rows, model_width),
@@ -367,7 +533,6 @@
     resid_low = resid_all.reshape(padded, model_width)[:tokens_here]
     layer_out = layer_all.reshape(padded, model_width)[:tokens_here].astype(f32)
 
-    local_attn_out = jnp.einsum("rh,rd->hd", context, resid_low, preferred_element_type=f32)
     context_grad = jnp.einsum(
         "rd,hd->rh", resid_low, attention_out, preferred_element_type=f32
     ).astype(bf16)
@@ -393,38 +558,46 @@
         jnp.einsum("rh,dh->rd", grads_flat[k], attention_in[k], preferred_element_type=f32)
         for k in range(3)
     )
-    (first_parts,) = scattered(
-        [pad_rows(partial_first).astype(bf16).reshape(cuts, rows, model_width)], 5
-    )
-    local_attn_in = jnp.stack(
-        [
-            jnp.einsum("rd,rh->dh", first, part, preferred_element_type=f32)
-            for part in grads_flat
-        ]
-    )
     local_first_gain = jnp.sum(partial_first * normed1, axis=0)
     local_first_bias = jnp.sum(partial_first, axis=0)
+    members = lax.axis_size("dp") * owners
+    share = model_width // members
     small = jnp.concatenate(
         [
             local_router.T,
             jnp.stack([local_first_gain, local_first_bias, local_second_gain, local_second_bias]),
         ]
-    ).astype(bf16)
-    small_sum = sent_and_summed(small, ("dp", "expert"), 1)
-    attention_in_grad = sent_and_summed(local_attn_in.astype(bf16), ("dp", "expert"), 1)
-    attention_out_grad = sent_and_summed(local_attn_out.astype(bf16), ("dp", "expert"), 1)
-
+    )
+    tall = rounded_up(small.shape[0], 8)
+    small = cut_along(small, 1, members)
+    small = jnp.pad(
+        small, ((0, 0), (0, tall - small.shape[1]), (0, rounded_up(share, 128) - share))
+    )
+    first_parts, small_parts = line_and_group(
+        pad_rows(partial_first).astype(bf16).reshape(cuts, rows, model_width), small, 5, False
+    )
     first_grad = jnp.sum(first_parts.astype(f32), axis=0)
+    small_sum = jnp.sum(small_parts, axis=0)
     normed1_rows, scale1_rows = normalize(my_rows(inputs).astype(f32))
     grad_rows = resid_grad + norm_back(first_grad, normed1_rows, scale1_rows, first_gain)
-    tall = rounded_up(small_sum.shape[0], 8)
-    wide = rounded_up(small_sum.shape[1], 128)
-    small_pad = jnp.pad(
-        small_sum, ((0, tall - small_sum.shape[0]), (0, wide - small_sum.shape[1]))
-    )
-    grad_all, small_all = gathered([grad_rows.astype(bf16), small_pad], 6)
-    input_grad = grad_all.reshape(padded, model_width)[:tokens_here].astype(f32)
-    totals = jnp.sum(small_all[0], axis=0)[: small_sum.shape[0], : small_sum.shape[1]]
+    small_low = small_sum.astype(bf16)
+    small_low = jnp.pad(small_low, ((0, rounded_up(tall, 16) - tall), (0, model_width - small_low.shape[1])))
+    attention_cuts = jnp.stack(
+        [
+            jnp.einsum("rd,rh->dh", left, part, preferred_element_type=f32).astype(bf16)
+            for left, part in zip([first] * 3 + [resid_low], grads_flat + [context])
+        ],
+        axis=1,
+    ).reshape(members, share, 4, local_width)
+    sent_rows = jnp.concatenate([grad_rows.astype(bf16), small_low])
+    grad_all, attention_parts = line_and_group(
+        sent_rows, jnp.swapaxes(attention_cuts, 1, 2), 6, True
+    )
+    input_grad = grad_all[:, :rows].reshape(padded, model_width)[:tokens_here].astype(f32)
+    totals = jnp.sum(grad_all[:, rows:].astype(f32), axis=0)[:, :share]
+    attention_sums = jnp.sum(attention_parts.astype(f32), axis=0)
+    attention_in_grad = attention_sums[:3]
+    attention_out_grad = attention_sums[3].T
     return (
         layer_out,
         input_grad,

time: 247 us -> 191 us (0.77)
  matrix products: 32.9 us -> 10.5 us
  Pallas kernels: 93.9 us -> 115 us
  other arithmetic: 42.3 us -> 28.3 us
  between operations: 14.9 us -> 1.49 us
  local copies, waits for them, and re-layouts: 27.4 us -> 17.2 us
  waiting for transfers between devices: 15.8 us -> 7.09 us
  starting transfers between devices: 17.7 us -> 11 us
    pallas_call x0 -> x3, Pallas kernels: none -> 46.2 us  [the longest x2 38.4 us: line_and_group(): pl.pallas_call(functools.partial(ends_kernel, gather), out_shape=[jax.Sha...]
    dot_general x14 -> x4, matrix products: 22.4 us -> 0.96 us  [per_device(): jnp.einsum('rd,rh->dh', left, part, preferred_element_type=f32).astype(bf16)]
    pallas_call x3 -> x2, Pallas kernels: 51.3 us -> 37.1 us  [gathered(): pl.pallas_call(functools.partial(gather_kernel, count, forward), out_shap...]
    all_to_all x3 -> x1, waiting for transfers between devices: 12.6 us -> 0.01 us  [per_device(): lax.all_to_all(expert_cuts, 'dp', 0, 0, tiled=True).astype(f32)]
    pallas_call x3 -> x2, Pallas kernels: 42.5 us -> 31.3 us  [scattered(): pl.pallas_call(functools.partial(scatter_kernel, count), out_shape=[jax.S...]
    all_to_all x3 -> x1, starting transfers between devices: 11.7 us -> 5.25 us  [per_device(): lax.all_to_all(expert_cuts, 'dp', 0, 0, tiled=True).astype(f32)]
    convert_element_type x5, other arithmetic: 7.59 us -> 1.96 us  [the longest x1 0.86 us: per_device(): grad_all[:, :rows].reshape(padded, model_width)[:tokens_here].astype(f32)]
    ppermute x5, waiting for transfers between devices: 3.24 us -> 7.08 us  [shifted(): lax.ppermute(array, axis, [(d, (d + offset) % devices) for d in range(dev...]
  transfers between devices with their start and end apart: 10 -> 6, of which waited for: 2 -> 2; matrix products, arithmetic and copies ran while one was open for 35% -> 23% of each run, Pallas kernels for 38% -> 56%
where the time goes in v2:
time: 191 us; the launch traced here: 190 us
  Pallas kernels  115 us (60%)
  other arithmetic  28.3 us (15%)
  local copies, waits for them, and re-layouts  17.2 us (9%)
  starting transfers between devices  11 us (6%)
  matrix products  10.5 us (5%)
  waiting for transfers between devices  7.09 us (4%)
    pallas_call x2, Pallas kernels, line_and_group(): pl.pallas_call(functools.partial(ends_kernel, gather), out_shape=[jax.Sha...  38.4 us
    pallas_call x2, Pallas kernels, gathered(): pl.pallas_call(functools.partial(gather_kernel, count, forward), out_shap...  37.1 us
    pallas_call x2, Pallas kernels, scattered(): pl.pallas_call(functools.partial(scatter_kernel, count), out_shape=[jax.S...  31.3 us
    pallas_call x1, Pallas kernels, experts_block(): pl.pallas_call(functools.partial(experts_kernel, experts_all), out_shape=...  7.78 us
    unnamed x86, local copies, waits for them, and re-layouts  7.34 us
    ppermute x5, waiting for transfers between devices, shifted(): lax.ppermute(array, axis, [(d, (d + offset) % devices) for d in range(dev...  7.08 us
    ppermute x5, starting transfers between devices, shifted(): lax.ppermute(array, axis, [(d, (d + offset) % devices) for d in range(dev...  5.73 us
    all_to_all x1, starting transfers between devices, per_device(): lax.all_to_all(expert_cuts, 'dp', 0, 0, tiled=True).astype(f32)  5.25 us
  transfers between devices with their start and end apart: 6, of which 2 were waited for; matrix products, arithmetic and copies ran while one was open for 23% of the time, Pallas kernels for 56%

profile of v2, /device:TPU:0, one launch (start us, length us, event | category | flops | bytes accessed | tf_op | source)
XLA Modules:
  0.0 190.2 jit_solution(2330022781497956496)
XLA Ops:
  2.1 3.0 %collective-permute-start = (f32[2,224]{1,0:T(2,128)}, f32[2,224]{1,0:T(2,128)}, u32[]{:S(2)}, u32[]{:S(2)}) collective-permute-start(f32[2,224]{1,0:T(2,128)} %get-tuple-element.107), channel_id=1, source_target_pairs={{0,4},{4,0},{1,5},{5,1},{2,6},{6,2},{3,7},{7,3},{8,12},{12,8},{9,1... | collective-permute-start | bytes 5384 | tf_op jit(solution)/shard_map/ppermute | solution.py:282
  5.1 1.9 pad_bitcast_fusion
  8.0 1.2 fusion.12
  13.5 11.9 %scatter1.1 = bf16[4,56,768]{2,1,0:T(8,128)(2,1)} custom-call(bf16[4,56,768]{2,1,0:T(8,128)(2,1)} %bitcast.147), custom_call_target="tpu_custom_call" | custom-call | tf_op jit(solution)/shard_map/scatter1/pallas_call | solution.py:197
  29.1 17.8 %gather2.1 = bf16[2,4,56,768]{3,2,1,0:T(8,128)(2,1)} custom-call(bf16[56,768]{1,0:T(8,128)(2,1)} %add_convert_fusion.1.refs_0_), custom_call_target="tpu_custom_call" | custom-call | tf_op jit(solution)/shard_map/gather2/pallas_call | solution.py:267
  51.5 1.7 copy-done.4
  53.2 7.8 %experts.1 = (bf16[2,224,768]{2,1,0:T(8,128)(2,1)S(1)}, bf16[2,224,768]{2,1,0:T(8,128)(2,1)S(1)}, f32[2,224,128]{2,1,0:T(8,128)S(1)}, f32[2,224,128]{2,1,0:T(8,128)S(1)}, bf16[4,2,2,192,768]{4,3,2,1,0:T(8,128)(2,1)S(1)}) custom-call(s32[2,2,224]{2,1,0:T(2,128)S(1)} %fusion.45.slot_ref, f32[2,128]{1,0:T(2,128)S(1)} %compare_convert_fusion.spot_ref, ...), custom_call_target="tpu_custom_call" | custom-call | tf_op jit(solution)/shard_map/experts/pallas_call | solution.py:395
  61.0 2.2 %copy-done.1 = bf16[4,2,2,192,768]{4,3,2,1,0:T(8,128)(2,1)} copy-done((bf16[4,2,2,192,768]{4,3,2,1,0:T(8,128)(2,1)}, bf16[4,2,2,192,768]{4,3,2,1,0:T(8,128)(2,1)S(1)}, u32[]{:S(2)}) %copy-start.1) | copy-done | bytes 4718616
  63.8 1.6 collective-permute-start.3
  66.0 5.3 %all-to-all-start = ((bf16[4,2,2,192,768]{4,3,2,1,0:T(8,128)(2,1)}), bf16[4,2,2,192,768]{4,3,2,1,0:T(8,128)(2,1)}, u32[]{:S(2)}, u32[]{:S(2)}) async-start(bf16[4,2,2,192,768]{4,3,2,1,0:T(8,128)(2,1)} %copy-done.1), calls=%async_computation | async-start | bytes 9437184 | tf_op jit(solution)/shard_map/all_to_all | solution.py:507
  72.0 4.2 %collective-permute-done.3 = bf16[224,768]{1,0:T(8,128)(2,1)S(1)} collective-permute-done((bf16[224,768]{1,0:T(8,128)(2,1)S(1)}, bf16[224,768]{1,0:T(8,128)(2,1)S(1)}, u32[]{:S(2)}, u32[]{:S(2)}) %collective-permute-start.3) | collective-permute-done | bytes 344096 | tf_op jit(solution)/shard_map/ppermute | solution.py:282
  77.0 2.9 %collective-permute-done.2 = bf16[224,768]{1,0:T(8,128)(2,1)S(1)} collective-permute-done((bf16[224,768]{1,0:T(8,128)(2,1)S(1)}, bf16[224,768]{1,0:T(8,128)(2,1)S(1)}, u32[]{:S(2)}, u32[]{:S(2)}) %collective-permute-start.2) | collective-permute-done | bytes 344096 | tf_op jit(solution)/shard_map/ppermute | solution.py:282
  80.7 19.4 %scatter3.1 = (bf16[4,56,768]{2,1,0:T(8,128)(2,1)}, bf16[4,56,768]{2,1,0:T(8,128)(2,1)}, f32[4,56,128]{2,1,0:T(8,128)}) custom-call(bf16[4,56,768]{2,1,0:T(8,128)(2,1)} %bitcast.145, bf16[4,56,768]{2,1,0:T(8,128)(2,1)} %bitcast.144, f32[4,56,128]{2,1,0:T(8,128)} %bitcast.156), custom_call_target="tpu_custom_call" | custom-call | tf_op jit(solution)/shard_map/scatter3/pallas_call | solution.py:197
  105.1 19.4 %gather4.1 = (bf16[1,4,56,768]{3,2,1,0:T(8,128)(2,1)}, bf16[1,4,56,768]{3,2,1,0:T(8,128)(2,1)}) custom-call(bf16[56,768]{1,0:T(8,128)(2,1)} %get-tuple-element.91.refs_0_, bf16[56,768]{1,0:T(8,128)(2,1)} %get-tuple-element.101.refs_1_), custom_call_target="tpu_custom_call" | custom-call | tf_op jit(solution)/shard_map/gather4/pallas_call | solution.py:267
  124.5 1.3 convolution_convert_fusion.8
  129.0 1.2 fusion.16
  130.2 1.2 convolution_add_fusion.1
  131.5 1.3 fusion.48
  134.5 13.1 %ends5.1 = (bf16[4,56,768]{2,1,0:T(8,128)(2,1)}, f32[8,8,128]{2,1,0:T(8,128)}) custom-call(bf16[4,56,768]{2,1,0:T(8,128)(2,1)} %bitcast.146, f32[8,8,128]{2,1,0:T(8,128)} %pad.40.refs_1_), custom_call_target="tpu_custom_call" | custom-call | tf_op jit(solution)/shard_map/ends5/pallas_call | solution.py:154
  150.5 1.5 maximum_bitcast_fusion.refs_1_
  152.0 25.3 %ends6.1 = (bf16[4,72,768]{2,1,0:T(8,128)(2,1)}, bf16[8,4,96,192]{3,2,1,0:T(8,128)(2,1)}) custom-call(bf16[72,768]{1,0:T(8,128)(2,1)} %fusion.41.refs_0_, bf16[8,4,96,192]{3,2,1,0:T(8,128)(2,1)} %maximum_bitcast_fusion.refs_1_), custom_call_target="tpu_custom_call" | custom-call | tf_op jit(solution)/shard_map/ends6/pallas_call | solution.py:154
  178.3 1.8 convert_reduce_fusion.1
  185.3 3.3 %convert_reduce_fusion = f32[2,2,192,768]{3,2,1,0:T(8,128)S(1)} fusion(bf16[4,2,2,192,768]{4,3,2,1,0:T(8,128)(2,1)} %all-to-all-done), kind=kLoop, calls=%fused_computation | loop fusion | flops 4128768 | bytes 7077888 | tf_op jit(solution)/shard_map/reduce_sum | solution.py:506
  188.6 1.6 slice_bitcast_fusion
  (173 shorter events, 37.2 us)
Async XLA Ops:
  0.6 11.8 %copy-start = (bf16[192,768]{1,0:T(8,128)(2,1)S(1)}, bf16[192,768]{1,0:T(8,128)(2,1)}, u32[]{:S(2)}) copy-start(bf16[192,768]{1,0:T(8,128)(2,1)} %param.17) | copy-start | bytes 884740
  0.7 8.6 %copy-start.13 = (bf16[197,768]{1,0:T(8,128)(2,1)S(1)}, bf16[197,768]{1,0:T(8,128)(2,1)}, u32[]{:S(2)}) copy-start(bf16[197,768]{1,0:T(8,128)(2,1)} %param.13) | copy-start | bytes 907780
  0.7 8.6 %copy-start.32 = (f32[768]{0:T(1024)S(1)}, f32[768]{0:T(1024)}, u32[]{:S(2)}) copy-start(f32[768]{0:T(1024)} %param.14) | copy-start | bytes 9220
  0.7 8.8 %copy-start.23 = (bf16[3,768,192]{1,2,0:T(8,128)(2,1)S(1)}, bf16[3,768,192]{1,2,0:T(8,128)(2,1)}, u32[]{:S(2)}) copy-start(bf16[3,768,192]{1,2,0:T(8,128)(2,1)} %param.16) | copy-start | bytes 2654212
  2.1 46.8 %collective-permute-start = (f32[2,224]{1,0:T(2,128)}, f32[2,224]{1,0:T(2,128)}, u32[]{:S(2)}, u32[]{:S(2)}) collective-permute-start(f32[2,224]{1,0:T(2,128)} %get-tuple-element.107), channel_id=1, source_target_pairs={{0,4},{4,0},{1,5},{5,1},{2,6},{6,2},{3,7},{7,3},{8,12},{12,8},{9,1... | collective-permute-start | bytes 5384 | tf_op jit(solution)/shard_map/ppermute | solution.py:282
  6.9 43.4 %collective-permute-start.1 = (bf16[224,768]{1,0:T(8,128)(2,1)}, bf16[224,768]{1,0:T(8,128)(2,1)}, u32[]{:S(2)}, u32[]{:S(2)}) collective-permute-start(bf16[224,768]{1,0:T(8,128)(2,1)} %get-tuple-element.100), channel_id=1, source_target_pairs={{0,4},{4,0},{1,5},{5,1},{2,6},{6,2},{3,7},{7,3},{8,12},{12,8},{9,1... | collective-permute-start | bytes 1032200 | tf_op jit(solution)/shard_map/ppermute | solution.py:282
  11.8 16.5 %copy-start.31 = (f32[768]{0:T(1024)S(1)}, f32[768]{0:T(1024)}, u32[]{:S(2)}) copy-start(f32[768]{0:T(1024)} %param.18) | copy-start | bytes 9220
  11.8 16.5 %copy-start.39 = (f32[768]{0:T(1024)S(1)}, f32[768]{0:T(1024)}, u32[]{:S(2)}) copy-start(f32[768]{0:T(1024)} %param.19) | copy-start | bytes 9220
  13.5 33.4 %copy-start.30 = (f32[768,4]{0,1:T(4,128)S(1)}, f32[768,4]{0,1:T(4,128)}, u32[]{:S(2)}) copy-start(f32[768,4]{0,1:T(4,128)} %param.20) | copy-start | bytes 36868
  29.1 22.4 %copy-start.3 = (bf16[2,768,768]{2,1,0:T(8,128)(2,1)S(1)}, bf16[2,768,768]{2,1,0:T(8,128)(2,1)}, u32[]{:S(2)}) copy-start(bf16[2,768,768]{2,1,0:T(8,128)(2,1)} %in_ref.1) | copy-start | bytes 7077892
  63.1 8.2 %collective-permute-start.4 = (f32[224,128]{1,0:T(8,128)S(1)}, f32[224,128]{1,0:T(8,128)S(1)}, u32[]{:S(2)}, u32[]{:S(2)}) collective-permute-start(f32[224,128]{1,0:T(8,128)S(1)} %slice_bitcast_fusion.4), channel_id=1, source_target_pairs={{0,4},{4,0},{1,5},{5,1},{2,6},{6,2},{3,7},{7,3},{8,12},{12,8},{9,1... | collective-permute-start | bytes 344072 | tf_op jit(solution)/shard_map/ppermute | solution.py:282
  63.8 12.4 %collective-permute-start.3 = (bf16[224,768]{1,0:T(8,128)(2,1)S(1)}, bf16[224,768]{1,0:T(8,128)(2,1)S(1)}, u32[]{:S(2)}, u32[]{:S(2)}) collective-permute-start(bf16[224,768]{1,0:T(8,128)(2,1)S(1)} %slice_bitcast_fusion.2), channel_id=1, source_target_pairs={{0,4},{4,0},{1,5},{5,1},{2,6},{6,2},{3,7},{7,3},{8,12},{12,8},{9,1... | collective-permute-start | bytes 1032200 | tf_op jit(solution)/shard_map/ppermute | solution.py:282
  65.4 14.5 %collective-permute-start.2 = (bf16[224,768]{1,0:T(8,128)(2,1)S(1)}, bf16[224,768]{1,0:T(8,128)(2,1)S(1)}, u32[]{:S(2)}, u32[]{:S(2)}) collective-permute-start(bf16[224,768]{1,0:T(8,128)(2,1)S(1)} %slice_bitcast_fusion.3), channel_id=1, source_target_pairs={{0,4},{4,0},{1,5},{5,1},{2,6},{6,2},{3,7},{7,3},{8,12},{12,8},{9,1... | collective-permute-start | bytes 1032200 | tf_op jit(solution)/shard_map/ppermute | solution.py:282
  66.0 10.2 %copy-start.8 = (bf16[2,224,768]{2,1,0:T(8,128)(2,1)S(1)}, bf16[2,224,768]{2,1,0:T(8,128)(2,1)}, u32[]{:S(2)}) copy-start(bf16[2,224,768]{2,1,0:T(8,128)(2,1)} %copy-done.7) | copy-start | bytes 2064388
  66.0 119.3 %all-to-all-start = ((bf16[4,2,2,192,768]{4,3,2,1,0:T(8,128)(2,1)}), bf16[4,2,2,192,768]{4,3,2,1,0:T(8,128)(2,1)}, u32[]{:S(2)}, u32[]{:S(2)}) async-start(bf16[4,2,2,192,768]{4,3,2,1,0:T(8,128)(2,1)} %copy-done.1), calls=%async_computation | async-start | bytes 9437184 | tf_op jit(solution)/shard_map/all_to_all | solution.py:507
  71.3 8.6 %copy-start.6 = (bf16[2,224,768]{2,1,0:T(8,128)(2,1)S(1)}, bf16[2,224,768]{2,1,0:T(8,128)(2,1)}, u32[]{:S(2)}) copy-start(bf16[2,224,768]{2,1,0:T(8,128)(2,1)} %copy-done.5) | copy-start | bytes 2064388
  77.0 26.3 %copy-start.36 = (f32[56]{0:T(128)S(1)}, f32[56]{0:T(128)}, u32[]{:S(2)}) copy-start(f32[56]{0:T(128)} %copy-done.35) | copy-start | bytes 676
  80.7 23.6 %copy-start.19 = (bf16[197,768]{1,0:T(8,128)(2,1)S(1)}, bf16[197,768]{1,0:T(8,128)(2,1)}, u32[]{:S(2)}) copy-start(bf16[197,768]{1,0:T(8,128)(2,1)} %param.25) | copy-start | bytes 907780
  102.1 23.7 %copy-start.12 = (f32[3,197,197]{1,2,0:T(8,128)S(1)}, f32[3,197,197]{1,2,0:T(8,128)}, u32[]{:S(2)}) copy-start(f32[3,197,197]{1,2,0:T(8,128)} %copy-done.11) | copy-start | bytes 1397128
  103.3 22.7 %copy-start.18 = (bf16[3,64,197]{2,1,0:T(8,128)(2,1)S(1)}, bf16[3,64,197]{2,1,0:T(8,128)(2,1)}, u32[]{:S(2)}) copy-start(bf16[3,64,197]{2,1,0:T(8,128)(2,1)} %copy-done.17) | copy-start | bytes 226948
  104.3 21.8 %copy-start.22 = (bf16[197,192]{0,1:T(8,128)(2,1)S(1)}, bf16[197,192]{0,1:T(8,128)(2,1)}, u32[]{:S(2)}) copy-start(bf16[197,192]{0,1:T(8,128)(2,1)} %copy-done.21) | copy-start | bytes 226948
  105.1 21.3 %copy-start.27 = (bf16[197,192]{0,1:T(8,128)(2,1)S(1)}, bf16[197,192]{0,1:T(8,128)(2,1)}, u32[]{:S(2)}) copy-start(bf16[197,192]{0,1:T(8,128)(2,1)} %copy-done.26) | copy-start | bytes 226948
  131.5 18.0 %copy-start.34 = (f32[56]{0:T(128)S(1)}, f32[56]{0:T(128)}, u32[]{:S(2)}) copy-start(f32[56]{0:T(128)} %copy-done.33) | copy-start | bytes 676
  131.5 18.0 %copy-start.37 = (f32[56]{0:T(128)S(1)}, f32[56]{0:T(128)}, u32[]{:S(2)}) copy-start(f32[56]{0:T(128)} %get-tuple-element.112) | copy-start | bytes 676
  (24 other events, 56.6 us)

commit v3 on v2

--- a/solution.py
+++ b/solution.py
@@ -529,9 +529,8 @@
     local_second_gain = jnp.sum(second_grad * normed2, axis=0)
     local_second_bias = jnp.sum(second_grad, axis=0)
     resid_grad = grad_out + norm_back(second_grad, normed2, scale2, second_gain)
-    resid_all, layer_all = gathered([resid_grad.astype(bf16), layer_rows.astype(bf16)], 4)
+    (resid_all,) = gathered([resid_grad.astype(bf16)], 4)
     resid_low = resid_all.reshape(padded, model_width)[:tokens_here]
-    layer_out = layer_all.reshape(padded, model_width)[:tokens_here].astype(f32)
 
     context_grad = jnp.einsum(
         "rd,hd->rh", resid_low, attention_out, preferred_element_type=f32
@@ -589,12 +588,13 @@
         ],
         axis=1,
     ).reshape(members, share, 4, local_width)
-    sent_rows = jnp.concatenate([grad_rows.astype(bf16), small_low])
+    sent_rows = jnp.concatenate([grad_rows.astype(bf16), layer_rows.astype(bf16), small_low])
     grad_all, attention_parts = line_and_group(
         sent_rows, jnp.swapaxes(attention_cuts, 1, 2), 6, True
     )
     input_grad = grad_all[:, :rows].reshape(padded, model_width)[:tokens_here].astype(f32)
-    totals = jnp.sum(grad_all[:, rows:].astype(f32), axis=0)[:, :share]
+    layer_out = grad_all[:, rows : 2 * rows].reshape(padded, model_width)[:tokens_here].astype(f32)
+    totals = jnp.sum(grad_all[:, 2 * rows :].astype(f32), axis=0)[:, :share]
     attention_sums = jnp.sum(attention_parts.astype(f32), axis=0)
     attention_in_grad = attention_sums[:3]
     attention_out_grad = attention_sums[3].T

time: 191 us -> 183 us (0.958)
  Pallas kernels: 115 us -> 108 us
    pallas_call x2, Pallas kernels: 37.1 us -> 31.2 us  [gathered(): pl.pallas_call(functools.partial(gather_kernel, count, forward), out_shap...]
    unnamed x86 -> x90, local copies, waits for them, and re-layouts: 7.34 us -> 7.02 us
  transfers between devices with their start and end apart: 6 -> 6, of which waited for: 2 -> 2; matrix products, arithmetic and copies ran while one was open for 23% -> 23% of each run, Pallas kernels for 56% -> 55%
where the time goes in v3:
time: 183 us; the launch traced here: 182 us
  Pallas kernels  108 us (59%)
  other arithmetic  27.4 us (15%)
  local copies, waits for them, and re-layouts  15.9 us (9%)
  matrix products  11.5 us (6%)
  starting transfers between devices  11 us (6%)
  waiting for transfers between devices  7.1 us (4%)
    pallas_call x2, Pallas kernels, line_and_group(): pl.pallas_call(functools.partial(ends_kernel, gather), out_shape=[jax.Sha...  37.3 us
    pallas_call x2, Pallas kernels, scattered(): pl.pallas_call(functools.partial(scatter_kernel, count), out_shape=[jax.S...  31.3 us
    pallas_call x2, Pallas kernels, gathered(): pl.pallas_call(functools.partial(gather_kernel, count, forward), out_shap...  31.2 us
    pallas_call x1, Pallas kernels, experts_block(): pl.pallas_call(functools.partial(experts_kernel, experts_all), out_shape=...  7.77 us
    ppermute x5, waiting for transfers between devices, shifted(): lax.ppermute(array, axis, [(d, (d + offset) % devices) for d in range(dev...  7.1 us
    unnamed x90, local copies, waits for them, and re-layouts  7.02 us
    ppermute x5, starting transfers between devices, shifted(): lax.ppermute(array, axis, [(d, (d + offset) % devices) for d in range(dev...  5.73 us
    all_to_all x1, starting transfers between devices, per_device(): lax.all_to_all(expert_cuts, 'dp', 0, 0, tiled=True).astype(f32)  5.25 us
  transfers between devices with their start and end apart: 6, of which 2 were waited for; matrix products, arithmetic and copies ran while one was open for 23% of the time, Pallas kernels for 55%

profile of v3, /device:TPU:0, one launch (start us, length us, event | category | flops | bytes accessed | tf_op | source)
XLA Modules:
  0.0 181.9 jit_solution(9359296404966195423)
XLA Ops:
  2.1 3.0 %collective-permute-start = (f32[2,224]{1,0:T(2,128)}, f32[2,224]{1,0:T(2,128)}, u32[]{:S(2)}, u32[]{:S(2)}) collective-permute-start(f32[2,224]{1,0:T(2,128)} %get-tuple-element.105), channel_id=1, source_target_pairs={{0,4},{4,0},{1,5},{5,1},{2,6},{6,2},{3,7},{7,3},{8,12},{12,8},{9,1... | collective-permute-start | bytes 5384 | tf_op jit(solution)/shard_map/ppermute | solution.py:282
  5.1 1.9 %pad_bitcast_fusion = (bf16[1,224,768]{2,1,0:T(8,128)(2,1)}, bf16[224,768]{1,0:T(8,128)(2,1)}) fusion(bf16[197,768]{1,0:T(8,128)(2,1)} %param.25), kind=kLoop, calls=%fused_computation.130 | loop fusion | bytes 990720 | tf_op jit(solution)/shard_map/stack | solution.py:287
  13.5 11.9 %scatter1.1 = bf16[4,56,768]{2,1,0:T(8,128)(2,1)} custom-call(bf16[4,56,768]{2,1,0:T(8,128)(2,1)} %bitcast.147), custom_call_target="tpu_custom_call" | custom-call | tf_op jit(solution)/shard_map/scatter1/pallas_call | solution.py:197
  28.8 17.8 %gather2.1 = bf16[2,4,56,768]{3,2,1,0:T(8,128)(2,1)} custom-call(bf16[56,768]{1,0:T(8,128)(2,1)} %add_convert_fusion.1.refs_0_), custom_call_target="tpu_custom_call" | custom-call | tf_op jit(solution)/shard_map/gather2/pallas_call | solution.py:267
  51.2 1.7 copy-done.4
  52.9 7.8 %experts.1 = (bf16[2,224,768]{2,1,0:T(8,128)(2,1)S(1)}, bf16[2,224,768]{2,1,0:T(8,128)(2,1)S(1)}, f32[2,224,128]{2,1,0:T(8,128)S(1)}, f32[2,224,128]{2,1,0:T(8,128)S(1)}, bf16[4,2,2,192,768]{4,3,2,1,0:T(8,128)(2,1)S(1)}) custom-call(s32[2,2,224]{2,1,0:T(2,128)S(1)} %fusion.45.slot_ref, f32[2,128]{1,0:T(2,128)S(1)} %compare_convert_fusion.spot_ref, ...), custom_call_target="tpu_custom_call" | custom-call | tf_op jit(solution)/shard_map/experts/pallas_call | solution.py:395
  60.7 2.2 %copy-done.1 = bf16[4,2,2,192,768]{4,3,2,1,0:T(8,128)(2,1)} copy-done((bf16[4,2,2,192,768]{4,3,2,1,0:T(8,128)(2,1)}, bf16[4,2,2,192,768]{4,3,2,1,0:T(8,128)(2,1)S(1)}, u32[]{:S(2)}) %copy-start.1) | copy-done | bytes 4718616
  63.5 1.6 collective-permute-start.3
  65.7 5.3 %all-to-all-start = ((bf16[4,2,2,192,768]{4,3,2,1,0:T(8,128)(2,1)}), bf16[4,2,2,192,768]{4,3,2,1,0:T(8,128)(2,1)}, u32[]{:S(2)}, u32[]{:S(2)}) async-start(bf16[4,2,2,192,768]{4,3,2,1,0:T(8,128)(2,1)} %copy-done.1), calls=%async_computation | async-start | bytes 9437184 | tf_op jit(solution)/shard_map/all_to_all | solution.py:507
  71.7 4.2 %collective-permute-done.3 = bf16[224,768]{1,0:T(8,128)(2,1)S(1)} collective-permute-done((bf16[224,768]{1,0:T(8,128)(2,1)S(1)}, bf16[224,768]{1,0:T(8,128)(2,1)S(1)}, u32[]{:S(2)}, u32[]{:S(2)}) %collective-permute-start.3) | collective-permute-done | bytes 344096 | tf_op jit(solution)/shard_map/ppermute | solution.py:282
  76.7 2.9 %collective-permute-done.2 = bf16[224,768]{1,0:T(8,128)(2,1)S(1)} collective-permute-done((bf16[224,768]{1,0:T(8,128)(2,1)S(1)}, bf16[224,768]{1,0:T(8,128)(2,1)S(1)}, u32[]{:S(2)}, u32[]{:S(2)}) %collective-permute-start.2) | collective-permute-done | bytes 344096 | tf_op jit(solution)/shard_map/ppermute | solution.py:282
  80.4 19.4 %scatter3.1 = (bf16[4,56,768]{2,1,0:T(8,128)(2,1)}, bf16[4,56,768]{2,1,0:T(8,128)(2,1)}, f32[4,56,128]{2,1,0:T(8,128)}) custom-call(bf16[4,56,768]{2,1,0:T(8,128)(2,1)} %bitcast.145, bf16[4,56,768]{2,1,0:T(8,128)(2,1)} %bitcast.144, f32[4,56,128]{2,1,0:T(8,128)} %bitcast.159), custom_call_target="tpu_custom_call" | custom-call | tf_op jit(solution)/shard_map/scatter3/pallas_call | solution.py:197
  104.8 13.4 %gather4.1 = bf16[1,4,56,768]{3,2,1,0:T(8,128)(2,1)} custom-call(bf16[56,768]{1,0:T(8,128)(2,1)} %get-tuple-element.87.refs_0_), custom_call_target="tpu_custom_call" | custom-call | tf_op jit(solution)/shard_map/gather4/pallas_call | solution.py:267
  118.1 1.2 convolution_convert_fusion.8
  119.4 1.2 convolution_convert_fusion.1
  122.0 1.2 fusion.17
  124.9 1.2 convolution_add_fusion.1
  126.1 1.3 fusion.48
  129.2 11.5 %ends5.1 = (bf16[4,56,768]{2,1,0:T(8,128)(2,1)}, f32[8,8,128]{2,1,0:T(8,128)}) custom-call(bf16[4,56,768]{2,1,0:T(8,128)(2,1)} %bitcast.146, f32[8,8,128]{2,1,0:T(8,128)} %pad.40.refs_1_), custom_call_target="tpu_custom_call" | custom-call | tf_op jit(solution)/shard_map/ends5/pallas_call | solution.py:154
  143.6 1.5 maximum_bitcast_fusion.refs_1_
  145.0 25.8 %ends6.1 = (bf16[4,128,768]{2,1,0:T(8,128)(2,1)}, bf16[8,4,96,192]{3,2,1,0:T(8,128)(2,1)}) custom-call(bf16[128,768]{1,0:T(8,128)(2,1)} %fusion.32.refs_0_, bf16[8,4,96,192]{3,2,1,0:T(8,128)(2,1)} %maximum_bitcast_fusion.refs_1_), custom_call_target="tpu_custom_call" | custom-call | tf_op jit(solution)/shard_map/ends6/pallas_call | solution.py:154
  170.9 1.8 convert_reduce_fusion.1
  177.1 3.3 %convert_reduce_fusion = f32[2,2,192,768]{3,2,1,0:T(8,128)S(1)} fusion(bf16[4,2,2,192,768]{4,3,2,1,0:T(8,128)(2,1)} %all-to-all-done), kind=kLoop, calls=%fused_computation | loop fusion | flops 4128768 | bytes 7077888 | tf_op jit(solution)/shard_map/reduce_sum | solution.py:506
  180.4 1.6 slice_bitcast_fusion
  (177 shorter events, 36.0 us)
Async XLA Ops:
  0.6 11.8 %copy-start = (bf16[192,768]{1,0:T(8,128)(2,1)S(1)}, bf16[192,768]{1,0:T(8,128)(2,1)}, u32[]{:S(2)}) copy-start(bf16[192,768]{1,0:T(8,128)(2,1)} %param.17) | copy-start | bytes 884740
  0.7 8.6 %copy-start.13 = (bf16[197,768]{1,0:T(8,128)(2,1)S(1)}, bf16[197,768]{1,0:T(8,128)(2,1)}, u32[]{:S(2)}) copy-start(bf16[197,768]{1,0:T(8,128)(2,1)} %param.13) | copy-start | bytes 907780
  0.7 8.8 %copy-start.24 = (bf16[3,768,192]{1,2,0:T(8,128)(2,1)S(1)}, bf16[3,768,192]{1,2,0:T(8,128)(2,1)}, u32[]{:S(2)}) copy-start(bf16[3,768,192]{1,2,0:T(8,128)(2,1)} %param.16) | copy-start | bytes 2654212
  2.1 46.5 %collective-permute-start = (f32[2,224]{1,0:T(2,128)}, f32[2,224]{1,0:T(2,128)}, u32[]{:S(2)}, u32[]{:S(2)}) collective-permute-start(f32[2,224]{1,0:T(2,128)} %get-tuple-element.105), channel_id=1, source_target_pairs={{0,4},{4,0},{1,5},{5,1},{2,6},{6,2},{3,7},{7,3},{8,12},{12,8},{9,1... | collective-permute-start | bytes 5384 | tf_op jit(solution)/shard_map/ppermute | solution.py:282
  6.9 43.1 %collective-permute-start.1 = (bf16[224,768]{1,0:T(8,128)(2,1)}, bf16[224,768]{1,0:T(8,128)(2,1)}, u32[]{:S(2)}, u32[]{:S(2)}) collective-permute-start(bf16[224,768]{1,0:T(8,128)(2,1)} %get-tuple-element.98), channel_id=1, source_target_pairs={{0,4},{4,0},{1,5},{5,1},{2,6},{6,2},{3,7},{7,3},{8,12},{12,8},{9,1... | collective-permute-start | bytes 1032200 | tf_op jit(solution)/shard_map/ppermute | solution.py:282
  11.8 16.2 %copy-start.31 = (f32[768]{0:T(1024)S(1)}, f32[768]{0:T(1024)}, u32[]{:S(2)}) copy-start(f32[768]{0:T(1024)} %param.18) | copy-start | bytes 9220
  11.8 16.2 %copy-start.41 = (f32[768]{0:T(1024)S(1)}, f32[768]{0:T(1024)}, u32[]{:S(2)}) copy-start(f32[768]{0:T(1024)} %param.19) | copy-start | bytes 9220
  13.5 33.1 %copy-start.30 = (f32[768,4]{0,1:T(4,128)S(1)}, f32[768,4]{0,1:T(4,128)}, u32[]{:S(2)}) copy-start(f32[768,4]{0,1:T(4,128)} %param.20) | copy-start | bytes 36868
  27.5 23.7 %copy-start.37 = (f32[56]{0:T(128)}, f32[56]{0:T(128)S(1)}, u32[]{:S(2)}) copy-start(f32[56]{0:T(128)S(1)} %add_rsqrt_fusion.2) | copy-start | bytes 676
  28.8 22.4 %copy-start.3 = (bf16[2,768,768]{2,1,0:T(8,128)(2,1)S(1)}, bf16[2,768,768]{2,1,0:T(8,128)(2,1)}, u32[]{:S(2)}) copy-start(bf16[2,768,768]{2,1,0:T(8,128)(2,1)} %in_ref.1) | copy-start | bytes 7077892
  62.8 8.2 %collective-permute-start.4 = (f32[224,128]{1,0:T(8,128)S(1)}, f32[224,128]{1,0:T(8,128)S(1)}, u32[]{:S(2)}, u32[]{:S(2)}) collective-permute-start(f32[224,128]{1,0:T(8,128)S(1)} %slice_bitcast_fusion.4), channel_id=1, source_target_pairs={{0,4},{4,0},{1,5},{5,1},{2,6},{6,2},{3,7},{7,3},{8,12},{12,8},{9,1... | collective-permute-start | bytes 344072 | tf_op jit(solution)/shard_map/ppermute | solution.py:282
  63.5 12.4 %collective-permute-start.3 = (bf16[224,768]{1,0:T(8,128)(2,1)S(1)}, bf16[224,768]{1,0:T(8,128)(2,1)S(1)}, u32[]{:S(2)}, u32[]{:S(2)}) collective-permute-start(bf16[224,768]{1,0:T(8,128)(2,1)S(1)} %slice_bitcast_fusion.2), channel_id=1, source_target_pairs={{0,4},{4,0},{1,5},{5,1},{2,6},{6,2},{3,7},{7,3},{8,12},{12,8},{9,1... | collective-permute-start | bytes 1032200 | tf_op jit(solution)/shard_map/ppermute | solution.py:282
  65.1 14.5 %collective-permute-start.2 = (bf16[224,768]{1,0:T(8,128)(2,1)S(1)}, bf16[224,768]{1,0:T(8,128)(2,1)S(1)}, u32[]{:S(2)}, u32[]{:S(2)}) collective-permute-start(bf16[224,768]{1,0:T(8,128)(2,1)S(1)} %slice_bitcast_fusion.3), channel_id=1, source_target_pairs={{0,4},{4,0},{1,5},{5,1},{2,6},{6,2},{3,7},{7,3},{8,12},{12,8},{9,1... | collective-permute-start | bytes 1032200 | tf_op jit(solution)/shard_map/ppermute | solution.py:282
  65.7 10.2 %copy-start.8 = (bf16[2,224,768]{2,1,0:T(8,128)(2,1)S(1)}, bf16[2,224,768]{2,1,0:T(8,128)(2,1)}, u32[]{:S(2)}) copy-start(bf16[2,224,768]{2,1,0:T(8,128)(2,1)} %copy-done.7) | copy-start | bytes 2064388
  65.7 111.3 %all-to-all-start = ((bf16[4,2,2,192,768]{4,3,2,1,0:T(8,128)(2,1)}), bf16[4,2,2,192,768]{4,3,2,1,0:T(8,128)(2,1)}, u32[]{:S(2)}, u32[]{:S(2)}) async-start(bf16[4,2,2,192,768]{4,3,2,1,0:T(8,128)(2,1)} %copy-done.1), calls=%async_computation | async-start | bytes 9437184 | tf_op jit(solution)/shard_map/all_to_all | solution.py:507
  71.0 8.6 %copy-start.6 = (bf16[2,224,768]{2,1,0:T(8,128)(2,1)S(1)}, bf16[2,224,768]{2,1,0:T(8,128)(2,1)}, u32[]{:S(2)}) copy-start(bf16[2,224,768]{2,1,0:T(8,128)(2,1)} %copy-done.5) | copy-start | bytes 2064388
  76.7 26.2 %copy-start.38 = (f32[56]{0:T(128)S(1)}, f32[56]{0:T(128)}, u32[]{:S(2)}) copy-start(f32[56]{0:T(128)} %copy-done.37) | copy-start | bytes 676
  80.4 23.6 %copy-start.19 = (bf16[197,768]{1,0:T(8,128)(2,1)S(1)}, bf16[197,768]{1,0:T(8,128)(2,1)}, u32[]{:S(2)}) copy-start(bf16[197,768]{1,0:T(8,128)(2,1)} %param.25) | copy-start | bytes 907780
  102.8 16.5 %copy-start.18 = (bf16[3,64,197]{2,1,0:T(8,128)(2,1)S(1)}, bf16[3,64,197]{2,1,0:T(8,128)(2,1)}, u32[]{:S(2)}) copy-start(bf16[3,64,197]{2,1,0:T(8,128)(2,1)} %copy-done.17) | copy-start | bytes 226948
  104.0 16.7 %copy-start.12 = (f32[3,197,197]{1,2,0:T(8,128)S(1)}, f32[3,197,197]{1,2,0:T(8,128)}, u32[]{:S(2)}) copy-start(f32[3,197,197]{1,2,0:T(8,128)} %copy-done.11) | copy-start | bytes 1397128
  104.8 16.2 %copy-start.23 = (bf16[197,192]{0,1:T(8,128)(2,1)S(1)}, bf16[197,192]{0,1:T(8,128)(2,1)}, u32[]{:S(2)}) copy-start(bf16[197,192]{0,1:T(8,128)(2,1)} %copy-done.22) | copy-start | bytes 226948
  126.1 16.4 %copy-start.36 = (f32[56]{0:T(128)S(1)}, f32[56]{0:T(128)}, u32[]{:S(2)}) copy-start(f32[56]{0:T(128)} %copy-done.35) | copy-start | bytes 676
  126.1 16.4 %copy-start.39 = (f32[56]{0:T(128)S(1)}, f32[56]{0:T(128)}, u32[]{:S(2)}) copy-start(f32[56]{0:T(128)} %get-tuple-element.110) | copy-start | bytes 676
  127.4 15.4 %copy-start.29 = (bf16[56,768]{1,0:T(8,128)(2,1)S(1)}, bf16[56,768]{1,0:T(8,128)(2,1)}, u32[]{:S(2)}) copy-start(bf16[56,768]{1,0:T(8,128)(2,1)} %get-tuple-element.99) | copy-start | bytes 258052
  (26 other events, 66.3 us)
